TPU v7x, 512 devices: a whole 4x8x8 slice. The times are simulated.
512 devices in a mesh: blade: 256 (over z, y, x), inst: 2 (over core).
Axes of the slice: x: 4, y: 8, z: 8, core: 2. Of those that a mesh axis runs over, the one named last changes fastest.
Arguments:
- tangent_seed: float32 [256, 5, 24, 1024], P('blade', None, 'inst'), may hold values from -6 to 6
- adjoint_seed: float32 [256, 5, 24, 1024], P('blade', None, 'inst'), may hold values from -6 to 6
- jacobian: bfloat16 [256, 24, 25, 1024], P('blade', 'inst'), may hold values from -1 to 4
- precond: bfloat16 [256, 24, 25, 1024], P('blade', 'inst'), may hold values from -1 to 4
- upwind: float32 [256, 1024], P('blade'), may hold values from 0.2 to 1
- up_weight: float32 [256, 256], P('blade'), may hold values from 0.3 to 1.2
- bottom_face_strength: float32 [256, 256], P('blade'), may hold values from 0.3 to 1.2
- up_cells: int32 [256], replicated, may hold values from 0 to 1023, as said below
- lo_cells: int32 [256], replicated, may hold values from 0 to 1023, as said below
- phase_index: int32 [11], replicated, may hold values from 0 to 255
Outputs:
- tangent_out: float32 [256, 5, 24, 1024], P('blade', None, 'inst')
- adjoint_out: float32 [256, 5, 24, 1024], P('blade', None, 'inst')
Inputs may be any that keep to these rules, and one draw needn't show every extreme that they name: `up_cells`: entry f of the table is one of the cells 4 f to 4 f + 3. `lo_cells`: entry f of the table is one of the cells 4 f to 4 f + 3.
All inputs are finite; a program needn't handle non-finite values.
Results may differ from a plain program's by a relative error of at most 0.0003.
Values sent between devices are 32-bit elements; how exact they have to be, the bound alone decides.
No kernel may reach another device: no remote copies, remote signals or barrier semaphores. Data moves between devices by JAX's collectives and lax.ppermute only.
A program may use at most 64 MiB of HBM per device.

v0:
```python
import jax
import jax.numpy as jnp
from jax import lax
from jax.sharding import PartitionSpec as P

SNAPSHOT_COUNT = 24
NH = 11


OMEGA = 0.15


def passed_along(block, axis, distance):
    devices = range(lax.axis_size(axis))
    route = [((i - distance) % len(devices), i) for i in devices]
    return lax.ppermute(block, axis, route)


def spectral(phase_index, passages):
    sampled_moments = jnp.arange(SNAPSHOT_COUNT, dtype=jnp.int32)
    snapshot_displacement = sampled_moments[:, None] - sampled_moments[None, :]
    orders = jnp.arange(1, NH + 1, dtype=jnp.int32)
    wrapped = (
        jnp.mod(orders[:, None, None] * snapshot_displacement[None, :, :], SNAPSHOT_COUNT).astype(
            jnp.float32
        )
        / SNAPSHOT_COUNT
    )
    weights = orders.astype(jnp.float32)[:, None, None]
    skewed = -(2.0 / SNAPSHOT_COUNT) * jnp.sum(weights * jnp.sin(2.0 * jnp.pi * wrapped), axis=0)
    derivative = 0.5 * skewed - 0.5 * skewed.T
    phase_angle = phase_index.astype(jnp.float32)[:, None, None] / passages
    parity = 1.0 - 2.0 * jnp.mod(snapshot_displacement, 2).astype(jnp.float32)
    rotation = (1.0 + parity) / SNAPSHOT_COUNT + 2.0 / SNAPSHOT_COUNT * jnp.sum(
        jnp.cos(2.0 * jnp.pi * (wrapped - phase_angle)), axis=0
    )
    return (derivative, rotation)


def block_apply(blocks, vector):
    variables = vector.shape[1]
    result_rows = []
    for row_index in range(variables):
        summed = blocks[:, :, row_index * variables, :] * vector[:, 0]
        for column_index in range(1, variables):
            summed = (
                summed
                + blocks[:, :, row_index * variables + column_index, :] * vector[:, column_index]
            )
        result_rows.append(summed)
    return jnp.stack(result_rows, axis=1)


def block_apply_t(blocks, vector):
    variables = vector.shape[1]
    result_rows = []
    for column_index in range(variables):
        summed = blocks[:, :, column_index, :] * vector[:, 0]
        for row_index in range(1, variables):
            summed = (
                summed
                + blocks[:, :, row_index * variables + column_index, :] * vector[:, row_index]
            )
        result_rows.append(summed)
    return jnp.stack(result_rows, axis=1)


def instance_mix(matrix, vector):
    return jnp.einsum("ts,pvsc->pvtc", matrix, vector, precision=lax.Precision.HIGHEST)


def cell_mask(cells_table):
    face_count = cells_table.shape[0]
    within = cells_table - 4 * jnp.arange(face_count, dtype=jnp.int32)
    spread = jnp.repeat(within, 4)
    slot_in_group = jnp.mod(jnp.arange(4 * face_count, dtype=jnp.int32), 4)
    return (spread == slot_in_group).astype(jnp.float32)


def face_pick(vector, mask):
    lead = vector.shape[:-1]
    picked = (vector * mask).reshape(lead + (vector.shape[-1] // 4, 4))
    return jnp.sum(picked, axis=-1)


def face_spread(values, mask):
    return jnp.repeat(values, 4, axis=-1) * mask


def regroup(vector, lo_mask, up_mask, derivative, rotation):
    lo_face = face_pick(vector, lo_mask)
    up_face = face_pick(vector, up_mask)
    own_count = vector.shape[2]
    first_row = lax.axis_index("inst") * own_count
    own_deriv = lax.dynamic_slice_in_dim(derivative, first_row, own_count, 0)
    own_rot = lax.dynamic_slice_in_dim(rotation, first_row, own_count, 0)
    own_rot_t = lax.dynamic_slice_in_dim(rotation.T, first_row, own_count, 0)
    return (
        instance_mix(own_deriv, lax.all_gather(vector, "inst", axis=2, tiled=True)),
        instance_mix(own_rot, lax.all_gather(lo_face, "inst", axis=2, tiled=True)),
        instance_mix(own_rot_t, lax.all_gather(up_face, "inst", axis=2, tiled=True)),
    )


def cycle_faces(next_source, previous_source_term):
    from_next = jnp.concatenate([next_source[1:], passed_along(next_source, "blade", -1)], axis=0)
    from_prev = jnp.concatenate(
        [passed_along(previous_source_term, "blade", 1), previous_source_term[:-1]], axis=0
    )
    return (from_next, from_prev)


def on_device(
    tangent_seed,
    adjoint_seed,
    jacobian,
    precond,
    upwind,
    up_weight,
    bottom_face_strength,
    up_cells,
    lo_cells,
    phase_index,
):
    passages = tangent_seed.shape[0] * lax.axis_size("blade")
    derivative, rotation = spectral(phase_index, passages)
    up_mask = cell_mask(up_cells)
    lo_mask = cell_mask(lo_cells)
    dual_field = block_apply_t(precond, adjoint_seed)
    negated = -dual_field
    up_scale = up_weight[:, None, None, :]
    lo_scale = bottom_face_strength[:, None, None, :]
    timed_tan, lo_tan, up_tan = regroup(tangent_seed, lo_mask, up_mask, derivative, rotation)
    next_tan, previous_tangent = cycle_faces(lo_tan, up_tan)
    timed_adj, lo_adj, up_adj = regroup(negated, lo_mask, up_mask, derivative, rotation)
    next_adj, prev_adj = cycle_faces(-lo_scale * lo_adj, -up_scale * up_adj)
    shifted = jnp.pad(tangent_seed[..., :-1], ((0, 0), (0, 0), (0, 0), (1, 0)))
    applied = (
        block_apply(jacobian, tangent_seed) - upwind[:, None, None, :] * shifted + OMEGA * timed_tan
    )
    applied = (
        applied
        - face_spread(up_scale * next_tan, up_mask)
        - face_spread(lo_scale * previous_tangent, lo_mask)
    )
    tangent_out = block_apply(precond, applied)
    shifted = jnp.pad(
        (upwind[:, None, None, :] * dual_field)[..., 1:], ((0, 0), (0, 0), (0, 0), (0, 1))
    )
    adjoint_out = block_apply_t(jacobian, dual_field) - shifted + OMEGA * timed_adj
    adjoint_out = adjoint_out - face_spread(prev_adj, lo_mask) - face_spread(next_adj, up_mask)
    return (tangent_out, adjoint_out)


def solution(mesh):
    in_specs = (
        P("blade", None, "inst", None),
        P("blade", None, "inst", None),
        P("blade", "inst", None, None),
        P("blade", "inst", None, None),
        P("blade", None),
        P("blade", None),
        P("blade", None),
        P(),
        P(),
        P(),
    )
    out_specs = (P("blade", None, "inst", None), P("blade", None, "inst", None))
    return jax.shard_map(
        on_device, mesh=mesh, in_specs=in_specs, out_specs=out_specs, check_vma=False
    )
```

profile of v0, /device:TPU:1, one launch (start us, length us, event | category | flops | bytes accessed | tf_op | source)
XLA Modules:
  0.0 108.2 jit_solution(11999192427864549714)
XLA Ops:
  2.5 1.8 %fusion.170 = (f32[1,5,12,1024]{3,2,1,0:T(8,128)S(1)}, f32[1,5,12,1024]{3,2,1,0:T(8,128)S(1)}, f32[1,5,12,1024]{3,2,1,0:T(8,128)}) fusion(f32[1,5,12,1024]{3,0,2,1:T(1,128)} %param.10, f32[1024]{0:T(1024)S(1)} %get-tuple-element.88, f32[1024]{0:T(1024)S(1)} %get-tuple-element.89), kind=kLoop, calls=%fused_computation.354 | loop fusion | flops 122880 | bytes 991232 | tf_op args[0]
  4.3 1.7 %copy.312 = f32[1,5,12,1024]{2,3,1,0:T(8,128)S(1)} copy(f32[1,5,12,1024]{3,2,1,0:T(8,128)} %get-tuple-element.77) | data formatting | bytes 491520 | tf_op jit(solution)/shard_map/mul | solution.py:82
  6.0 2.9 %reduce_sum.66 = f32[5,12,256]{1,2,0:T(8,128)} reduce(f32[5,12,256,4]{1,3,2,0:T(4,128)S(1)} %bitcast.467, f32[]{:T(128)} %constant.66.clone.1), dimensions={3}, to_apply=%region_3.4 | reduce | flops 46080 | bytes 307204 | tf_op jit(solution)/shard_map/reduce_sum | solution.py:83
  10.3 8.5 %all-gather.1 = f32[5,24,256]{2,0,1:T(8,128)S(1)} all-gather(f32[5,12,256]{2,0,1:T(8,128)S(1)} %copy.313), channel_id=3, replica_groups=mesh['blade'=256,'inst'=2] {'inst'}, dimensions={1}, use_global_device_ids=true | all-gather | bytes 184320 | tf_op jit(solution)/shard_map/all_gather | solution.py:101
  18.8 1.7 %multiply_reduce_fusion.2 = (f32[24,24]{1,0:T(8,128)}, f32[24,24]{1,0:T(8,128)S(1)}) fusion(s32[24,24]{1,0:T(8,128)S(1)} %iota_subtract_fusion, s32[11]{0:T(128)S(1)} %get-tuple-element.90, f32[11]{0:T(128)S(1)} %get-tuple-element.91, f32[11]{0:T(128)S(1)} %convert_multiply_fusion.75), kind=kLoop, calls=%fused_computation.31 | loop fusion | flops 93888 | bytes 7044 | tf_op jit(solution)/shard_map/reduce_sum | solution.py:30
  21.5 1.9 %collective-permute-start.1 = (f32[1,5,12,256]{3,2,1,0:T(8,128)}, f32[1,5,12,256]{3,2,1,0:T(8,128)}, u32[]{:S(2)}, u32[]{:S(2)}) collective-permute-start(f32[1,5,12,256]{3,2,1,0:T(8,128)} %convolution_bitcast_fusion.2), channel_id=1, source_target_pairs={{510,0},{0,2},{2,4},{4,6},{6,8},{8,10},{10,12},{12,14},{14,16},{16... | collective-permute-start | bytes 184328 | tf_op jit(solution)/shard_map/ppermute | solution.py:16
  24.2 2.9 %reduce_sum.63 = f32[5,12,256]{1,2,0:T(8,128)} reduce(f32[5,12,256,4]{1,3,2,0:T(4,128)S(1)} %bitcast.466, f32[]{:T(128)} %constant.66.clone.1), dimensions={3}, to_apply=%region_1.2 | reduce | flops 46080 | bytes 307204 | tf_op jit(solution)/shard_map/reduce_sum | solution.py:83
  28.5 1.9 %all-gather = f32[5,24,256]{2,0,1:T(8,128)S(1)} all-gather(f32[5,12,256]{2,0,1:T(8,128)S(1)} %copy.307), channel_id=2, replica_groups=mesh['blade'=256,'inst'=2] {'inst'}, dimensions={1}, use_global_device_ids=true | all-gather | bytes 184320 | tf_op jit(solution)/shard_map/all_gather | solution.py:100
  31.4 10.7 %collective-permute-start = (f32[1,5,12,256]{3,2,1,0:T(8,128)}, f32[1,5,12,256]{3,2,1,0:T(8,128)}, u32[]{:S(2)}, u32[]{:S(2)}) collective-permute-start(f32[1,5,12,256]{3,2,1,0:T(8,128)} %convolution_bitcast_fusion.3), channel_id=1, source_target_pairs={{2,0},{4,2},{6,4},{8,6},{10,8},{12,10},{14,12},{16,14},{18,16},{20... | collective-permute-start | bytes 184328 | tf_op jit(solution)/shard_map/ppermute | solution.py:16
  42.1 2.1 %fusion.168 = (bf16[1,12,1,1024]{3,2,1,0:T(2,128)(2,1)S(1)}, bf16[1,12,1,1024]{3,2,1,0:T(2,128)(2,1)S(1)}, bf16[1,12,1,1024]{3,2,1,0:T(2,128)(2,1)S(1)}, bf16[1,...) fusion(bf16[1,12,25,1024]{3,2,1,0:T(8,128)(2,1)} %param.12), kind=kLoop, calls=%fused_computation.352 | loop fusion | bytes 294912 | tf_op jit(solution)/shard_map/slice | solution.py:44
  44.1 4.7 %fusion.167 = (bf16[1,12,1,1024]{3,2,1,0:T(2,128)(2,1)}, bf16[1,12,1,1024]{3,2,1,0:T(2,128)(2,1)}, bf16[1,12,1,1024]{3,2,1,0:T(2,128)(2,1)}, bf16[1,12,1,1024]{3...) fusion(bf16[1,12,25,1024]{3,2,1,0:T(8,128)(2,1)} %param.12), kind=kLoop, calls=%fused_computation.351 | loop fusion | bytes 933888 | tf_op jit(solution)/shard_map/slice | solution.py:48
  55.3 2.4 %all-gather.3 = f32[5,24,256]{2,0,1:T(8,128)S(1)} all-gather(f32[5,12,256]{2,0,1:T(8,128)S(1)} %copy.368), channel_id=5, replica_groups=mesh['blade'=256,'inst'=2] {'inst'}, dimensions={1}, use_global_device_ids=true | all-gather | bytes 184320 | tf_op jit(solution)/shard_map/all_gather | solution.py:100
  58.6 3.6 %collective-permute-start.3 = (f32[1,5,12,256]{3,2,1,0:T(8,128)}, f32[1,5,12,256]{3,2,1,0:T(8,128)}, u32[]{:S(2)}, u32[]{:S(2)}) collective-permute-start(f32[1,5,12,256]{3,2,1,0:T(8,128)} %fusion.11), channel_id=1, source_target_pairs={{2,0},{4,2},{6,4},{8,6},{10,8},{12,10},{14,12},{16,14},{18,16},{20... | collective-permute-start | bytes 184328 | tf_op jit(solution)/shard_map/ppermute | solution.py:16
  62.3 2.4 %all-gather.2 = f32[5,24,256]{2,0,1:T(8,128)S(1)} all-gather(f32[5,12,256]{2,0,1:T(8,128)S(1)} %copy.361), channel_id=4, replica_groups=mesh['blade'=256,'inst'=2] {'inst'}, dimensions={1}, use_global_device_ids=true | all-gather | bytes 184320 | tf_op jit(solution)/shard_map/all_gather | solution.py:101
  65.6 2.0 %collective-permute-start.2 = (f32[1,5,12,256]{3,2,1,0:T(8,128)}, f32[1,5,12,256]{3,2,1,0:T(8,128)}, u32[]{:S(2)}, u32[]{:S(2)}) collective-permute-start(f32[1,5,12,256]{3,2,1,0:T(8,128)} %fusion.9), channel_id=1, source_target_pairs={{510,0},{0,2},{2,4},{4,6},{6,8},{8,10},{10,12},{12,14},{14,16},{16... | collective-permute-start | bytes 184328 | tf_op jit(solution)/shard_map/ppermute | solution.py:16
  67.7 2.2 %all_gather.18 = f32[1,5,24,1024]{3,0,1,2:T(1,128)S(1)} all-gather(f32[1,5,12,1024]{3,0,1,2:T(1,128)S(1)} %copy.303), channel_id=1, replica_groups=mesh['blade'=256,'inst'=2] {'inst'}, dimensions={2}, use_global_device_ids=true | all-gather | bytes 737280 | tf_op jit(solution)/shard_map/all_gather | solution.py:99
  77.0 2.5 %all_gather.21 = f32[1,5,24,1024]{3,0,1,2:T(1,128)} all-gather(f32[1,5,12,1024]{3,0,1,2:T(1,128)S(1)} %copy.347), channel_id=1, replica_groups=mesh['blade'=256,'inst'=2] {'inst'}, dimensions={2}, use_global_device_ids=true | all-gather | bytes 737280 | tf_op jit(solution)/shard_map/all_gather | solution.py:99
  82.7 1.5 %broadcast_in_dim.48 = f32[5,12,256,4]{1,3,2,0:T(4,128)S(1)} broadcast(f32[5,12,256]{1,2,0:T(8,128)} %copy.316), dimensions={0,1,2} | broadcast | bytes 307200 | tf_op jit(solution)/shard_map/broadcast_in_dim | solution.py:87
  87.7 1.5 %broadcast_in_dim.21 = f32[5,12,256,4]{1,3,2,0:T(4,128)S(1)} broadcast(f32[5,12,256]{1,2,0:T(8,128)} %copy.309), dimensions={0,1,2} | broadcast | bytes 307200 | tf_op jit(solution)/shard_map/broadcast_in_dim | solution.py:87
  91.0 1.9 %fusion.4 = f32[1,5,12,1024]{3,2,1,0:T(8,128)S(1)} fusion(f32[1,5,24,1024]{3,0,1,2:T(1,128)S(1)} %all_gather.18, f32[1,5,12,1024]{3,2,1,0:T(8,128)} %copy.317, f32[1,5,12,1024]{3,2,1,0:T(8,128)} %copy.310, f32[1,5,12,1024]{3,2,1,0:T(8,128)} %copy-done.5, f32[1,5,12,1023]{3,2,1,0:T(8,128)S(1)} %bitcast.465, f32[1024]{0:T(1024)S(1)} %get-tuple-element.89, ...), kind=kOutput, calls=%fused_computation.6 | convolution fusion | flops 18186528 | bytes 1987476 | tf_op jit(solution)/shard_map/ts,pvsc->pvtc/dot_general | solution.py:69
  95.2 2.0 %copy.370 = f32[5,12,256]{1,2,0:T(8,128)} copy(f32[5,12,256]{2,1,0:T(8,128)} %bitcast.136) | data formatting | bytes 122880 | tf_op jit(solution)/shard_map/ppermute | solution.py:16
  100.3 2.0 %copy.364 = f32[5,12,256]{1,2,0:T(8,128)} copy(f32[5,12,256]{2,1,0:T(8,128)} %bitcast.132) | data formatting | bytes 122880 | tf_op jit(solution)/shard_map/ppermute | solution.py:16
  102.3 1.6 %broadcast_in_dim.50 = f32[5,12,256,4]{1,3,2,0:T(4,128)S(1)} broadcast(f32[5,12,256]{1,2,0:T(8,128)} %copy.364), dimensions={0,1,2} | broadcast | bytes 307200 | tf_op jit(solution)/shard_map/broadcast_in_dim | solution.py:87
  105.5 1.7 %fusion.7 = f32[1,5,12,1024]{3,2,1,0:T(8,128)S(1)} fusion(f32[1,5,24,1024]{3,0,1,2:T(1,128)S(1)} %copy-done, f32[1,5,12,1024]{3,2,1,0:T(8,128)} %copy.371, f32[1,5,12,1024]{3,2,1,0:T(8,128)} %copy.365, f32[1,5,12,1024]{3,2,1,0:T(8,128)} %copy-done.4, f32[1,5,12,1023]{3,2,1,0:T(8,128)S(1)} %copy-done.2, f32[1024]{0:T(1024)S(1)} %get-tuple-element.89, ...), kind=kOutput, calls=%fused_computation.9 | convolution fusion | flops 18125088 | bytes 1826820 | tf_op jit(solution)/shard_map/ts,pvsc->pvtc/dot_general | solution.py:69
  (227 shorter events, 38.1 us)
Async XLA Ops:
  6.0 12.8 %copy-start.70 = (s32[11]{0:T(128)S(1)}, s32[11]{0:T(128)}, u32[]{:S(2)}) copy-start(s32[11]{0:T(128)} %param.19) | copy-start | bytes 136
  21.5 59.1 %collective-permute-start.1 = (f32[1,5,12,256]{3,2,1,0:T(8,128)}, f32[1,5,12,256]{3,2,1,0:T(8,128)}, u32[]{:S(2)}, u32[]{:S(2)}) collective-permute-start(f32[1,5,12,256]{3,2,1,0:T(8,128)} %convolution_bitcast_fusion.2), channel_id=1, source_target_pairs={{510,0},{0,2},{2,4},{4,6},{6,8},{8,10},{10,12},{12,14},{14,16},{16... | collective-permute-start | bytes 184328 | tf_op jit(solution)/shard_map/ppermute | solution.py:16
  27.0 21.8 %copy-start.1 = (bf16[1,12,25,1024]{3,2,1,0:T(8,128)(2,1)S(1)}, bf16[1,12,25,1024]{3,2,1,0:T(8,128)(2,1)}, u32[]{:S(2)}) copy-start(bf16[1,12,25,1024]{3,2,1,0:T(8,128)(2,1)} %param.13) | copy-start | bytes 1843204
  31.4 19.2 %copy-start.63 = (f32[1,5,12,1024]{3,0,2,1:T(1,128)S(1)}, f32[1,5,12,1024]{3,0,2,1:T(1,128)}, u32[]{:S(2)}) copy-start(f32[1,5,12,1024]{3,0,2,1:T(1,128)} %param.11) | copy-start | bytes 737284
  31.4 54.3 %collective-permute-start = (f32[1,5,12,256]{3,2,1,0:T(8,128)}, f32[1,5,12,256]{3,2,1,0:T(8,128)}, u32[]{:S(2)}, u32[]{:S(2)}) collective-permute-start(f32[1,5,12,256]{3,2,1,0:T(8,128)} %convolution_bitcast_fusion.3), channel_id=1, source_target_pairs={{2,0},{4,2},{6,4},{8,6},{10,8},{12,10},{14,12},{16,14},{18,16},{20... | collective-permute-start | bytes 184328 | tf_op jit(solution)/shard_map/ppermute | solution.py:16
  53.5 11.1 %copy-start.69 = (f32[1,256]{1,0:T(1,128)S(1)}, f32[1,256]{1,0:T(1,128)}, u32[]{:S(2)}) copy-start(f32[1,256]{1,0:T(1,128)} %param.15) | copy-start | bytes 3076
  53.5 14.1 %copy-start.3 = (f32[1,5,12,1024]{3,0,2,1:T(1,128)S(1)}, f32[1,5,12,1024]{3,0,2,1:T(1,128)}, u32[]{:S(2)}) copy-start(f32[1,5,12,1024]{3,0,2,1:T(1,128)} %param.10) | copy-start | bytes 737284
  54.4 16.9 %copy-start.50 = (bf16[1,12,1,1024]{3,2,1,0:T(2,128)(2,1)S(1)}, bf16[1,12,1,1024]{3,2,1,0:T(2,128)(2,1)}, u32[]{:S(2)}) copy-start(bf16[1,12,1,1024]{3,2,1,0:T(2,128)(2,1)} %get-tuple-element.60) | copy-start | bytes 73732
  54.4 16.9 %copy-start.54 = (bf16[1,12,1,1024]{3,2,1,0:T(2,128)(2,1)S(1)}, bf16[1,12,1,1024]{3,2,1,0:T(2,128)(2,1)}, u32[]{:S(2)}) copy-start(bf16[1,12,1,1024]{3,2,1,0:T(2,128)(2,1)} %get-tuple-element.61) | copy-start | bytes 73732
  54.6 17.6 %copy-start.49 = (bf16[1,12,1,1024]{3,2,1,0:T(2,128)(2,1)S(1)}, bf16[1,12,1,1024]{3,2,1,0:T(2,128)(2,1)}, u32[]{:S(2)}) copy-start(bf16[1,12,1,1024]{3,2,1,0:T(2,128)(2,1)} %get-tuple-element.55) | copy-start | bytes 73732
  54.6 17.6 %copy-start.53 = (bf16[1,12,1,1024]{3,2,1,0:T(2,128)(2,1)S(1)}, bf16[1,12,1,1024]{3,2,1,0:T(2,128)(2,1)}, u32[]{:S(2)}) copy-start(bf16[1,12,1,1024]{3,2,1,0:T(2,128)(2,1)} %get-tuple-element.56) | copy-start | bytes 73732
  54.7 17.6 %copy-start.60 = (bf16[1,12,1,1024]{3,2,1,0:T(2,128)(2,1)S(1)}, bf16[1,12,1,1024]{3,2,1,0:T(2,128)(2,1)}, u32[]{:S(2)}) copy-start(bf16[1,12,1,1024]{3,2,1,0:T(2,128)(2,1)} %get-tuple-element.57) | copy-start | bytes 73732
  54.9 18.2 %copy-start.56 = (bf16[1,12,1,1024]{3,2,1,0:T(2,128)(2,1)S(1)}, bf16[1,12,1,1024]{3,2,1,0:T(2,128)(2,1)}, u32[]{:S(2)}) copy-start(bf16[1,12,1,1024]{3,2,1,0:T(2,128)(2,1)} %get-tuple-element.48) | copy-start | bytes 73732
  55.3 18.7 %copy-start.48 = (bf16[1,12,1,1024]{3,2,1,0:T(2,128)(2,1)S(1)}, bf16[1,12,1,1024]{3,2,1,0:T(2,128)(2,1)}, u32[]{:S(2)}) copy-start(bf16[1,12,1,1024]{3,2,1,0:T(2,128)(2,1)} %get-tuple-element.50) | copy-start | bytes 73732
  55.3 18.7 %copy-start.52 = (bf16[1,12,1,1024]{3,2,1,0:T(2,128)(2,1)S(1)}, bf16[1,12,1,1024]{3,2,1,0:T(2,128)(2,1)}, u32[]{:S(2)}) copy-start(bf16[1,12,1,1024]{3,2,1,0:T(2,128)(2,1)} %get-tuple-element.51) | copy-start | bytes 73732
  55.3 18.7 %copy-start.59 = (bf16[1,12,1,1024]{3,2,1,0:T(2,128)(2,1)S(1)}, bf16[1,12,1,1024]{3,2,1,0:T(2,128)(2,1)}, u32[]{:S(2)}) copy-start(bf16[1,12,1,1024]{3,2,1,0:T(2,128)(2,1)} %get-tuple-element.52) | copy-start | bytes 73732
  58.6 36.7 %collective-permute-start.3 = (f32[1,5,12,256]{3,2,1,0:T(8,128)}, f32[1,5,12,256]{3,2,1,0:T(8,128)}, u32[]{:S(2)}, u32[]{:S(2)}) collective-permute-start(f32[1,5,12,256]{3,2,1,0:T(8,128)} %fusion.11), channel_id=1, source_target_pairs={{2,0},{4,2},{6,4},{8,6},{10,8},{12,10},{14,12},{16,14},{18,16},{20... | collective-permute-start | bytes 184328 | tf_op jit(solution)/shard_map/ppermute | solution.py:16
  62.3 12.7 %copy-start.55 = (bf16[1,12,1,1024]{3,2,1,0:T(2,128)(2,1)S(1)}, bf16[1,12,1,1024]{3,2,1,0:T(2,128)(2,1)}, u32[]{:S(2)}) copy-start(bf16[1,12,1,1024]{3,2,1,0:T(2,128)(2,1)} %get-tuple-element.47) | copy-start | bytes 73732
  65.6 10.3 %copy-start.47 = (bf16[1,12,1,1024]{3,2,1,0:T(2,128)(2,1)S(1)}, bf16[1,12,1,1024]{3,2,1,0:T(2,128)(2,1)}, u32[]{:S(2)}) copy-start(bf16[1,12,1,1024]{3,2,1,0:T(2,128)(2,1)} %get-tuple-element.45) | copy-start | bytes 73732
  65.6 10.3 %copy-start.51 = (bf16[1,12,1,1024]{3,2,1,0:T(2,128)(2,1)S(1)}, bf16[1,12,1,1024]{3,2,1,0:T(2,128)(2,1)}, u32[]{:S(2)}) copy-start(bf16[1,12,1,1024]{3,2,1,0:T(2,128)(2,1)} %get-tuple-element.46) | copy-start | bytes 73732
  65.6 10.3 %copy-start.58 = (bf16[1,12,1,1024]{3,2,1,0:T(2,128)(2,1)S(1)}, bf16[1,12,1,1024]{3,2,1,0:T(2,128)(2,1)}, u32[]{:S(2)}) copy-start(bf16[1,12,1,1024]{3,2,1,0:T(2,128)(2,1)} %copy-done.57) | copy-start | bytes 73732
  65.6 34.7 %collective-permute-start.2 = (f32[1,5,12,256]{3,2,1,0:T(8,128)}, f32[1,5,12,256]{3,2,1,0:T(8,128)}, u32[]{:S(2)}, u32[]{:S(2)}) collective-permute-start(f32[1,5,12,256]{3,2,1,0:T(8,128)} %fusion.9), channel_id=1, source_target_pairs={{510,0},{0,2},{2,4},{4,6},{6,8},{8,10},{10,12},{12,14},{14,16},{16... | collective-permute-start | bytes 184328 | tf_op jit(solution)/shard_map/ppermute | solution.py:16
  74.1 5.4 %copy-start.66 = (f32[1,1024]{1,0:T(1,128)S(1)}, f32[1,1024]{1,0:T(1,128)}, u32[]{:S(2)}) copy-start(f32[1,1024]{1,0:T(1,128)} %param.14) | copy-start | bytes 12292
  75.0 5.6 %copy-start.68 = (f32[1,256]{1,0:T(1,128)S(1)}, f32[1,256]{1,0:T(1,128)}, u32[]{:S(2)}) copy-start(f32[1,256]{1,0:T(1,128)} %param.16) | copy-start | bytes 3076
  (51 other events, 151.4 us)
where the time goes:
time: 110 us; the launch traced here: 108 us
  local copies, waits for them, and re-layouts  39.6 us (36%)
  other arithmetic  21.2 us (19%)
  blocking collectives  19.8 us (18%)
  starting transfers between devices  18.3 us (17%)
  matrix products  7.35 us (7%)
  between operations  1.95 us (2%)
    ppermute x4, starting transfers between devices, passed_along(): return lax.ppermute(block, axis, route)  18.3 us
    broadcast_in_dim x8, local copies, waits for them, and re-layouts, face_spread(): return jnp.repeat(values, 4, axis=-1) * mask  12.2 us
    all_gather x2, blocking collectives, regroup(): lax.all_gather(up_face, 'inst', axis=2, tiled=True)  10.8 us
    unnamed x13, other arithmetic  8.42 us
    dot_general x6, matrix products, instance_mix(): jnp.einsum('ts,pvsc->pvtc', matrix, vector, precision=lax.Precision.HIGHEST)  7.35 us
    reduce_sum x3, other arithmetic, face_pick(): return jnp.sum(picked, axis=-1)  6.04 us
    slice x2, local copies, waits for them, and re-layouts, block_apply(): blocks[:, :, row_index * variables + column_index, :]  5.68 us
    all_gather x2, blocking collectives, regroup(): lax.all_gather(vector, 'inst', axis=2, tiled=True)  4.67 us
  transfers between devices with their start and end apart: 4, of which 0 were waited for; matrix products, arithmetic and copies ran while one was open for 44% of the time, Pallas kernels for 0%

commit v1 on v0

v1 whole, which is shorter than its diff:
```python
import math

import jax
import jax.numpy as jnp
from jax import lax
from jax.experimental import pallas as pl
from jax.experimental.pallas import tpu as pltpu
from jax.sharding import PartitionSpec as P

SNAPS = 24
NH = 11
NV = 5
OWN = 12
OMEGA = 0.15
SUB, LANE = 8, 128
ROWS = NV * OWN
FIELD = 2 * ROWS
FACE_ROWS = 3 * OWN
MPITCH = OWN * 32
CHUNKS = 4
CHUNK = OWN // CHUNKS


def derivative_weights():
    weights = [0.0]
    for n in range(1, 12):
        total = sum(k * math.sin(2 * math.pi * ((k * n) % SNAPS) / SNAPS) for k in range(1, NH + 1))
        weights.append(-(2.0 / SNAPS) * total)
    return weights


DERIV = derivative_weights()


def passed_along(block, axis, distance):
    count = lax.axis_size(axis)
    route = [((i - distance) % count, i) for i in range(count)]
    return lax.ppermute(block, axis, route)


def lanes():
    return lax.broadcasted_iota(jnp.int32, (SUB, LANE), 1)


def sublanes():
    return lax.broadcasted_iota(jnp.int32, (SUB, LANE), 0)


def take(x, index):
    return jnp.take_along_axis(x, index, axis=1, mode="promise_in_bounds")


def quarters(row):
    first = jnp.broadcast_to(row[:, :LANE], (SUB, LANE))
    second = jnp.broadcast_to(row[:, LANE:], (SUB, LANE))
    sub = sublanes()
    both = jnp.where(sub < 4, first, second)
    return take(both, 32 * (sub & 3) + (lanes() & 31))


def wide(row):
    return jnp.concatenate([row[:, LANE * k : LANE * (k + 1)] for k in range(SUB)], axis=0)


def load_blocks(blocks, scratch, first, count):
    def body(t, carry):
        for k in range(SUB):
            tile = blocks[0, t, :, LANE * k : LANE * (k + 1)].astype(jnp.float32)
            scratch[pl.ds(pl.multiple_of(k * MPITCH + t * 32, 8), NV * NV), :] = tile
        return carry

    lax.fori_loop(first, first + count, body, 0)


def fetch(pairs, sems):
    copies = [pltpu.make_async_copy(src, dst, sems.at[n]) for n, (src, dst) in enumerate(pairs)]
    for copy in copies:
        copy.start()
    return copies


def fetch_blocks(blocks, scratch, sems):
    return fetch(
        [(blocks.at[:, pl.ds(CHUNK * n, CHUNK)], scratch.at[:, pl.ds(CHUNK * n, CHUNK)]) for n in range(CHUNKS)],
        sems,
    )


def block_row(scratch, t, ij):
    return scratch[pl.ds(t * 32 + ij, SUB, stride=MPITCH), :]


def packed(parts, quarter):
    result = parts[-1]
    for g in reversed(range(len(parts) - 1)):
        result = jnp.where(quarter == g, parts[g], result)
    return result


def dual_kernel(tangent, adjoint, precond, out, m_s, p_v, a_v, t_sem, p_sem):
    seeds = fetch([(adjoint, a_v), (tangent, out.at[pl.ds(0, ROWS)])], t_sem)
    chunks = fetch_blocks(precond, p_v, p_sem)

    def body(t, carry):
        seed = [a_v[i * OWN + t] for i in range(NV)]
        for j in range(NV):
            total = block_row(m_s, t, j) * seed[0]
            for i in range(1, NV):
                total = total + block_row(m_s, t, i * NV + j) * seed[i]
            out[ROWS + j * OWN + t] = total
        return carry

    for n in range(CHUNKS):
        chunks[n].wait()
        load_blocks(p_v, m_s, CHUNK * n, CHUNK)
        if n == 0:
            seeds[0].wait()
        lax.fori_loop(CHUNK * n, CHUNK * (n + 1), body, 0)
    seeds[1].wait()


def rotate_kernel(
    phase, gathered, up_weight, lo_weight, up_cells, lo_cells,
    up_out, lo_out, g_v, uw, lw, uc, lc, rho, u_s, l_s, sems,
):
    own = lax.axis_index("inst")
    copies = fetch(
        [(up_weight, uw), (lo_weight, lw), (up_cells, uc), (lo_cells, lc), (gathered, g_v)], sems
    )
    shape = (16, LANE)
    order = lax.broadcasted_iota(jnp.int32, shape, 0) + 1
    lag = lax.broadcasted_iota(jnp.int32, shape, 1)
    index = jnp.zeros(shape, jnp.int32)
    for k in range(NH):
        index = jnp.where(order == k + 1, phase[k], index)
    turns = (32 * order * (lag & 31) - 3 * index).astype(jnp.float32)
    turns = turns - 768.0 * jnp.floor(turns * (1.0 / 768.0) + 0.5)
    waves = jnp.where(order <= NH, jnp.cos(turns * (2.0 * math.pi / 768.0)), 0.0)
    parity = (1 - (lag[:1] & 1)).astype(jnp.float32)
    row = (2.0 / SNAPS) * (parity + jnp.sum(waves, axis=0, keepdims=True))
    for n in range(SNAPS):
        rho[n] = jnp.broadcast_to(row[:, n : n + 1], (SUB, LANE))
    for copy in copies[:4]:
        copy.wait()
    quarter = lanes() >> 5
    odd = (quarter & 1) == 1
    up_index = quarters(uc[...]) & (LANE - 1)
    lo_index = quarters(lc[...]) & (LANE - 1)
    even_rows = jnp.where(odd, lo_index, up_index)
    odd_rows = jnp.where(odd, up_index, lo_index)
    up_scale = quarters(uw[...])
    lo_scale = quarters(lw[...])
    up_mid = jnp.where(quarter == 0, 1.0, up_scale)
    lo_mid = jnp.where(quarter == 1, 1.0, lo_scale)
    copies[4].wait()

    def pick(n, carry):
        which = n // OWN
        t = n - OWN * which
        core = jnp.where(which == 0, own, 1 - own)
        rows = [
            take(g_v[core, q * OWN + t], odd_rows if q % 2 else even_rows) for q in range(2 * NV)
        ]
        swapped = [rows[q ^ 1] for q in range(2 * NV)]
        for j in range(3):
            u_s[j, n] = packed(rows[4 * j : 4 * j + 4], quarter)
            l_s[j, n] = packed(swapped[4 * j : 4 * j + 4], quarter)
        return carry

    lax.fori_loop(0, SNAPS, pick, 0)
    for result, source, sign, mid, last in (
        (up_out, u_s, -1, up_mid, up_scale),
        (lo_out, l_s, 1, lo_mid, lo_scale),
    ):
        for j in range(3):
            sums = [None] * OWN
            for s in range(SNAPS):
                x = source[j, s]
                for r in range(OWN):
                    term = rho[(sign * (r - s)) % SNAPS] * x
                    sums[r] = term if sums[r] is None else sums[r] + term
            for r in range(OWN):
                result[OWN * j + r] = sums[r] if j == 0 else sums[r] * (mid if j == 1 else last)


def local_kernel(gathered, jacobian, upwind, out, g_v, j_v, f_v, m_s, mix, g_sem, j_sem):
    own = lax.axis_index("inst")
    fields = fetch([(gathered, g_v), (upwind, f_v)], g_sem)
    chunks = fetch_blocks(jacobian, j_v, j_sem)
    fields[0].wait()

    for fld, sign in ((0, 1.0), (1, -1.0)):

        def mix_body(i, carry):
            base = (fld * NV + i) * OWN
            mine = [g_v[own, base + s] for s in range(OWN)]
            theirs = [g_v[1 - own, base + s] for s in range(OWN)]
            ring = mine + theirs
            for r in range(OWN):
                total = None
                for k in range(1, OWN):
                    term = (sign * OMEGA * DERIV[k]) * (ring[(r - k) % SNAPS] - ring[(r + k) % SNAPS])
                    total = term if total is None else total + term
                mix[base + r] = total
            return carry

        lax.fori_loop(0, NV, mix_body, 0)

    fields[1].wait()
    lane = lanes()
    cell = sublanes() * LANE + lane
    flow = jnp.where(cell == 0, 0.0, wide(f_v[...]))

    def body(t, carry):
        tangent = [g_v[own, i * OWN + t] for i in range(NV)]
        dual = [g_v[own, (NV + i) * OWN + t] for i in range(NV)]
        sums = [None] * NV
        dsums = [None] * NV
        for i in range(NV):
            for j in range(NV):
                m = block_row(m_s, t, i * NV + j)
                term = m * tangent[j]
                sums[i] = term if j == 0 else sums[i] + term
                term = m * dual[i]
                dsums[j] = term if i == 0 else dsums[j] + term
        for i in range(NV):
            x = pltpu.roll(tangent[i], 1, 1)
            x = jnp.where(lane == 0, pltpu.roll(x, 1, 0), x)
            out[i * OWN + t] = sums[i] - flow * x + mix[i * OWN + t]
            x = pltpu.roll(flow * dual[i], LANE - 1, 1)
            x = jnp.where(lane == LANE - 1, pltpu.roll(x, SUB - 1, 0), x)
            out[(NV + i) * OWN + t] = dsums[i] - x + mix[(NV + i) * OWN + t]
        return carry

    for n in range(CHUNKS):
        chunks[n].wait()
        load_blocks(j_v, m_s, CHUNK * n, CHUNK)
        lax.fori_loop(CHUNK * n, CHUNK * (n + 1), body, 0)


def final_kernel(
    partial, from_prev, from_next, m_s, up_weight, lo_weight, up_cells, lo_cells,
    tangent_out, adjoint_out, uw, lw, uc, lc, sems,
):
    for copy in fetch([(up_weight, uw), (lo_weight, lw), (up_cells, uc), (lo_cells, lc)], sems):
        copy.wait()
    lane = lanes()
    quarter = lane >> 5
    up_index = quarters(uc[...]) & (LANE - 1)
    lo_index = quarters(lc[...]) & (LANE - 1)
    up_hit = take(up_index, lane >> 2) == lane
    lo_hit = take(lo_index, lane >> 2) == lane
    up_scale = quarters(uw[...])
    lo_scale = quarters(lw[...])
    lo_mid = jnp.where(quarter == 0, lo_scale, 1.0)
    up_mid = jnp.where(quarter == 1, up_scale, 1.0)
    spots = [32 * g + (lane >> 2) for g in range(4)]

    def body(t, carry):
        prev = [from_prev[OWN * j + t] for j in range(3)]
        next_ = [from_next[OWN * j + t] for j in range(3)]
        prev = [prev[0] * lo_scale, prev[1] * lo_mid, prev[2]]
        next_ = [next_[0] * up_scale, next_[1] * up_mid, next_[2]]
        rows = []
        for q in range(2 * NV):
            low = take(prev[q // 4], spots[q % 4])
            high = take(next_[q // 4], spots[(q % 4) ^ 1])
            value = partial[q * OWN + t]
            value = value - jnp.where(lo_hit, low, 0.0)
            value = value - jnp.where(up_hit, high, 0.0)
            rows.append(value)
        for i in range(NV):
            total = block_row(m_s, t, i * NV) * rows[0]
            for j in range(1, NV):
                total = total + block_row(m_s, t, i * NV + j) * rows[j]
            tangent_out[i * OWN + t] = total
            adjoint_out[i * OWN + t] = rows[NV + i]
        return carry

    lax.fori_loop(0, OWN, body, 0)


def rows_of(count):
    return jax.ShapeDtypeStruct((count, SUB, LANE), jnp.float32)


BLOCK = (SUB * MPITCH, LANE)
BLOCKS = jax.ShapeDtypeStruct(BLOCK, jnp.float32)
ANY = pl.BlockSpec(memory_space=pl.ANY)
VMEM = pl.BlockSpec(memory_space=pltpu.VMEM)
SMEM = pl.BlockSpec(memory_space=pltpu.SMEM)


def held(shape, dtype=jnp.float32):
    return pltpu.VMEM(shape, dtype)


def sems(count):
    return pltpu.SemaphoreType.DMA((count,))


def call(kernel, in_specs, out_shape, scratch, name):
    return pl.pallas_call(
        kernel,
        in_specs=in_specs,
        out_shape=out_shape,
        scratch_shapes=scratch,
        compiler_params=pltpu.CompilerParams(vmem_limit_bytes=24 << 20),
        name=name,
    )


def on_device(
    tangent_seed,
    adjoint_seed,
    jacobian,
    precond,
    upwind,
    up_weight,
    bottom_face_strength,
    up_cells,
    lo_cells,
    phase_index,
):
    face = up_cells.shape[0]
    tables = (up_weight, bottom_face_strength, up_cells.reshape(1, face), lo_cells.reshape(1, face))
    table_scratch = [held((1, face)), held((1, face)), held((1, face), jnp.int32), held((1, face), jnp.int32)]
    rows = (ROWS, SUB, LANE)
    both = (2, FIELD, SUB, LANE)
    fields, precond_rows = call(
        dual_kernel,
        [ANY, ANY, ANY],
        (rows_of(FIELD), BLOCKS),
        [held(precond.shape, precond.dtype), held(rows), sems(2), sems(CHUNKS)],
        "dual",
    )(tangent_seed.reshape(rows), adjoint_seed.reshape(rows), precond)
    gathered = lax.all_gather(fields, "inst", axis=0, tiled=True).reshape(both)
    up_face, lo_face = call(
        rotate_kernel,
        [SMEM, ANY, ANY, ANY, ANY, ANY],
        (rows_of(FACE_ROWS), rows_of(FACE_ROWS)),
        [held(both), *table_scratch, held((SNAPS, SUB, LANE)), held((3, SNAPS, SUB, LANE)), held((3, SNAPS, SUB, LANE)), sems(5)],
        "rotate",
    )(phase_index, gathered, *tables)
    from_prev = passed_along(up_face, "blade", 1)
    from_next = passed_along(lo_face, "blade", -1)
    partial = call(
        local_kernel,
        [ANY, ANY, ANY],
        rows_of(FIELD),
        [held(both), held(jacobian.shape, jacobian.dtype), held(upwind.shape), held(BLOCK), held((FIELD, SUB, LANE)), sems(2), sems(CHUNKS)],
        "local",
    )(gathered, jacobian, upwind)
    tangent_out, adjoint_out = call(
        final_kernel,
        [VMEM, VMEM, VMEM, VMEM, ANY, ANY, ANY, ANY],
        (rows_of(ROWS), rows_of(ROWS)),
        [*table_scratch, sems(4)],
        "final",
    )(partial, from_prev, from_next, precond_rows, *tables)
    return tangent_out.reshape(tangent_seed.shape), adjoint_out.reshape(adjoint_seed.shape)


def solution(mesh):
    in_specs = (
        P("blade", None, "inst", None),
        P("blade", None, "inst", None),
        P("blade", "inst", None, None),
        P("blade", "inst", None, None),
        P("blade", None),
        P("blade", None),
        P("blade", None),
        P(),
        P(),
        P(),
    )
    out_specs = (P("blade", None, "inst", None), P("blade", None, "inst", None))
    return jax.shard_map(
        on_device, mesh=mesh, in_specs=in_specs, out_specs=out_specs, check_vma=False
    )
```

time: 110 us -> 37.3 us (0.34); the launches traced: 108 us -> 37.1 us
  local copies, waits for them, and re-layouts: 39.6 us -> 3.06 us
  other arithmetic: 21.2 us -> 0 us
  Pallas kernels: 0 us -> 11.9 us
  blocking collectives: 19.8 us -> 9.01 us
  matrix products: 7.35 us -> 0 us
  starting transfers between devices: 18.3 us -> 12.3 us
  between operations: 1.95 us -> 0.76 us
    broadcast_in_dim x10 -> x0, local copies, waits for them, and re-layouts: 12.4 us -> none  [the longest x8 12.2 us: face_spread(): return jnp.repeat(values, 4, axis=-1) * mask]
    pallas_call x0 -> x4, Pallas kernels: none -> 11.9 us  [the longest x1 3.79 us: on_device(): call(rotate_kernel, [SMEM, ANY, ANY, ANY, ANY, ANY], (rows_of(FACE_ROWS),...]
    all_gather x6 -> x1, blocking collectives: 19.8 us -> 9.01 us  [on_device(): gathered = lax.all_gather(fields, 'inst', axis=0, tiled=True).reshape(both)]
    unnamed x13 -> x0, other arithmetic: 8.42 us -> none
    slice x6 -> x0, local copies, waits for them, and re-layouts: 8.1 us -> none  [the longest x2 5.68 us: block_apply(): blocks[:, :, row_index * variables + column_index, :]]
    reduce_sum x4 -> x0, other arithmetic: 7.69 us -> none  [the longest x3 6.04 us: face_pick(): return jnp.sum(picked, axis=-1)]
    dot_general x6 -> x0, matrix products: 7.35 us -> none  [instance_mix(): jnp.einsum('ts,pvsc->pvtc', matrix, vector, precision=lax.Precision.HIGHEST)]
    ppermute x4 -> x2, starting transfers between devices: 18.3 us -> 12.3 us  [passed_along(): return lax.ppermute(block, axis, route)]
  transfers between devices with their start and end apart: 4 -> 2, of which waited for: 0 -> 0; matrix products, arithmetic and copies ran while one was open for 44% -> 0% of each run, Pallas kernels for 0% -> 8%
where the time goes in v1:
time: 37.3 us; the launch traced here: 37.1 us
  starting transfers between devices  12.3 us (33%)
  Pallas kernels  11.9 us (32%)
  blocking collectives  9.01 us (24%)
  local copies, waits for them, and re-layouts  3.06 us (8%)
  between operations  0.76 us (2%)
    ppermute x2, starting transfers between devices, passed_along(): return lax.ppermute(block, axis, route)  12.3 us
    all_gather x1, blocking collectives, on_device(): gathered = lax.all_gather(fields, 'inst', axis=0, tiled=True).reshape(both)  9.01 us
    pallas_call x1, Pallas kernels, on_device(): call(rotate_kernel, [SMEM, ANY, ANY, ANY, ANY, ANY], (rows_of(FACE_ROWS),...  3.79 us
    pallas_call x1, Pallas kernels, on_device(): call(local_kernel, [ANY, ANY, ANY], rows_of(FIELD), [held(both), held(jac...  3.11 us
    unnamed x20, local copies, waits for them, and re-layouts  3.06 us
    pallas_call x1, Pallas kernels, on_device(): call(dual_kernel, [ANY, ANY, ANY], (rows_of(FIELD), BLOCKS), [held(precon...  2.61 us
    pallas_call x1, Pallas kernels, on_device(): call(final_kernel, [VMEM, VMEM, VMEM, VMEM, ANY, ANY, ANY, ANY], (rows_of...  2.41 us
  transfers between devices with their start and end apart: 2, of which 0 were waited for; matrix products, arithmetic and copies ran while one was open for 0% of the time, Pallas kernels for 8%

profile of v1, /device:TPU:1, one launch (start us, length us, event | category | flops | bytes accessed | tf_op | source)
XLA Modules:
  0.0 37.1 jit_solution(5724610970671138639)
XLA Ops:
  0.6 0.0 copy-start.6
  0.6 0.0 copy-start.5
  0.7 0.0 copy-start.9
  0.7 0.0 copy-start.7
  0.7 0.0 copy-start
  0.7 1.1 %copy-done = bf16[1,12,25,1024]{3,2,1,0:T(8,128)(2,1)S(1)} copy-done((bf16[1,12,25,1024]{3,2,1,0:T(8,128)(2,1)S(1)}, bf16[1,12,25,1024]{3,2,1,0:T(8,128)(2,1)}, u32[]{:S(2)}) %copy-start) | copy-done | bytes 614424
  1.8 0.9 %copy-done.2 = f32[1,5,12,1024]{3,0,2,1:T(1,128)S(1)} copy-done((f32[1,5,12,1024]{3,0,2,1:T(1,128)S(1)}, f32[1,5,12,1024]{3,0,2,1:T(1,128)}, u32[]{:S(2)}) %copy-start.2) | copy-done | bytes 245784
  2.8 0.9 %copy-done.3 = f32[1,5,12,1024]{3,0,2,1:T(1,128)S(1)} copy-done((f32[1,5,12,1024]{3,0,2,1:T(1,128)S(1)}, f32[1,5,12,1024]{3,0,2,1:T(1,128)}, u32[]{:S(2)}) %copy-start.3) | copy-done | bytes 245784
  3.7 2.6 %dual.1 = (f32[120,8,128]{2,1,0:T(8,128)S(1)}, f32[3072,128]{1,0:T(8,128)S(1)}) custom-call(f32[60,8,128]{2,1,0:T(8,128)S(1)} %bitcast.9, f32[60,8,128]{2,1,0:T(8,128)S(1)} %bitcast.10, bf16[1,12,25,1024]{3,2,1,0:T(8,128)(2,1)S(1)} %copy-done), custom_call_target="tpu_custom_call" | custom-call | tf_op jit(solution)/shard_map/dual/pallas_call | solution.py:330
  6.3 9.0 %all_gather.3 = f32[240,8,128]{2,1,0:T(8,128)S(1)} all-gather(f32[120,8,128]{2,1,0:T(8,128)S(1)} %get-tuple-element.8), channel_id=1, replica_groups=mesh['blade'=256,'inst'=2] {'inst'}, dimensions={0}, use_global_device_ids=true | all-gather | bytes 1474560 | tf_op jit(solution)/shard_map/all_gather | solution.py:337
  15.4 0.0 copy-done.6
  15.4 0.0 copy-done.5
  15.4 0.0 copy-done.9
  15.4 0.0 copy-done.7
  15.4 0.0 copy-done.8
  15.4 3.8 %rotate.1 = (f32[36,8,128]{2,1,0:T(8,128)S(1)}, f32[36,8,128]{2,1,0:T(8,128)S(1)}) custom-call(s32[11]{0:T(128)S(1)} %copy-done.9, f32[2,120,8,128]{3,2,1,0:T(8,128)S(1)} %bitcast.7, f32[1,256]{1,0:T(1,128)S(1)} %copy-done.5, f32[1,256]{1,0:T(1,128)S(1)} %copy-done.6, s32[1,256]{1,0:T(1,128)S(1)} %bitcast.11, s32[1,256]{1,0:T(1,128)S(1)} %bitcast.13), custom_call_target="tpu_custom_call" | custom-call | tf_op jit(solution)/shard_map/rotate/pallas_call | solution.py:338
  19.2 1.9 %collective-permute-start = (f32[36,8,128]{2,1,0:T(8,128)S(1)}, f32[36,8,128]{2,1,0:T(8,128)S(1)}, u32[]{:S(2)}, u32[]{:S(2)}) collective-permute-start(f32[36,8,128]{2,1,0:T(8,128)S(1)} %get-tuple-element.9), channel_id=1, source_target_pairs={{510,0},{0,2},{2,4},{4,6},{6,8},{8,10},{10,12},{12,14},{14,16},{16... | collective-permute-start | bytes 442376 | tf_op jit(solution)/shard_map/ppermute | solution.py:38
  21.1 10.4 %collective-permute-start.1 = (f32[36,8,128]{2,1,0:T(8,128)S(1)}, f32[36,8,128]{2,1,0:T(8,128)S(1)}, u32[]{:S(2)}, u32[]{:S(2)}) collective-permute-start(f32[36,8,128]{2,1,0:T(8,128)S(1)} %get-tuple-element.10), channel_id=1, source_target_pairs={{2,0},{4,2},{6,4},{8,6},{10,8},{12,10},{14,12},{16,14},{18,16},{20... | collective-permute-start | bytes 442376 | tf_op jit(solution)/shard_map/ppermute | solution.py:38
  31.5 0.0 copy-done.1
  31.5 0.0 copy-done.4
  31.5 3.1 %local.1.partial = f32[120,8,128]{2,1,0:T(8,128)S(1)} custom-call(f32[2,120,8,128]{3,2,1,0:T(8,128)S(1)} %bitcast.8, bf16[1,12,25,1024]{3,2,1,0:T(8,128)(2,1)S(1)} %copy-done.1, f32[1,1024]{1,0:T(1,128)S(1)} %copy-done.4), custom_call_target="tpu_custom_call" | custom-call | tf_op jit(solution)/shard_map/local/pallas_call | solution.py:347
  34.7 0.0 collective-permute-done.from_prev
  34.7 0.0 collective-permute-done.1.from_next
  34.7 2.4 %final.1 = (f32[60,8,128]{2,1,0:T(8,128)}, f32[60,8,128]{2,1,0:T(8,128)}) custom-call(f32[120,8,128]{2,1,0:T(8,128)S(1)} %local.1.partial, f32[36,8,128]{2,1,0:T(8,128)S(1)} %collective-permute-done.from_prev, f32[36,8,128]{2,1,0:T(8,128)S(1)} %collective-permute-done.1.from_next, f32[3072,128]{1,0:T(8,128)S(1)} %get-tuple-element.11.m_s, ...), custom_call_target="tpu_custom_call" | custom-call | tf_op jit(solution)/shard_map/final/pallas_call | solution.py:354
  (5 shorter events, 0.0 us)
Async XLA Ops:
  0.6 14.7 %copy-start.6 = (f32[1,256]{1,0:T(1,128)S(1)}, f32[1,256]{1,0:T(1,128)}, u32[]{:S(2)}) copy-start(f32[1,256]{1,0:T(1,128)} %lo_weight.3) | copy-start | bytes 3076
  0.6 14.7 %copy-start.5 = (f32[1,256]{1,0:T(1,128)S(1)}, f32[1,256]{1,0:T(1,128)}, u32[]{:S(2)}) copy-start(f32[1,256]{1,0:T(1,128)} %up_weight.3) | copy-start | bytes 3076
  0.7 14.7 %copy-start.9 = (s32[11]{0:T(128)S(1)}, s32[11]{0:T(128)}, u32[]{:S(2)}) copy-start(s32[11]{0:T(128)} %phase.1) | copy-start | bytes 136
  0.7 14.7 %copy-start.7 = (s32[256]{0:T(256)S(1)}, s32[256]{0:T(256)}, u32[]{:S(2)}) copy-start(s32[256]{0:T(256)} %param.17) | copy-start | bytes 3076
  0.7 1.2 %copy-start = (bf16[1,12,25,1024]{3,2,1,0:T(8,128)(2,1)S(1)}, bf16[1,12,25,1024]{3,2,1,0:T(8,128)(2,1)}, u32[]{:S(2)}) copy-start(bf16[1,12,25,1024]{3,2,1,0:T(8,128)(2,1)} %precond.1) | copy-start | bytes 1843204
  1.8 0.9 %copy-start.2 = (f32[1,5,12,1024]{3,0,2,1:T(1,128)S(1)}, f32[1,5,12,1024]{3,0,2,1:T(1,128)}, u32[]{:S(2)}) copy-start(f32[1,5,12,1024]{3,0,2,1:T(1,128)} %param.10) | copy-start | bytes 737284
  2.8 0.9 %copy-start.3 = (f32[1,5,12,1024]{3,0,2,1:T(1,128)S(1)}, f32[1,5,12,1024]{3,0,2,1:T(1,128)}, u32[]{:S(2)}) copy-start(f32[1,5,12,1024]{3,0,2,1:T(1,128)} %param.11) | copy-start | bytes 737284
  3.7 11.7 %copy-start.8 = (s32[256]{0:T(256)S(1)}, s32[256]{0:T(256)}, u32[]{:S(2)}) copy-start(s32[256]{0:T(256)} %param.18) | copy-start | bytes 3076
  3.7 27.8 %copy-start.1 = (bf16[1,12,25,1024]{3,2,1,0:T(8,128)(2,1)S(1)}, bf16[1,12,25,1024]{3,2,1,0:T(8,128)(2,1)}, u32[]{:S(2)}) copy-start(bf16[1,12,25,1024]{3,2,1,0:T(8,128)(2,1)} %jacobian.1) | copy-start | bytes 1843204
  3.7 27.8 %copy-start.4 = (f32[1,1024]{1,0:T(1,128)S(1)}, f32[1,1024]{1,0:T(1,128)}, u32[]{:S(2)}) copy-start(f32[1,1024]{1,0:T(1,128)} %upwind.1) | copy-start | bytes 12292
  19.2 15.5 %collective-permute-start = (f32[36,8,128]{2,1,0:T(8,128)S(1)}, f32[36,8,128]{2,1,0:T(8,128)S(1)}, u32[]{:S(2)}, u32[]{:S(2)}) collective-permute-start(f32[36,8,128]{2,1,0:T(8,128)S(1)} %get-tuple-element.9), channel_id=1, source_target_pairs={{510,0},{0,2},{2,4},{4,6},{6,8},{8,10},{10,12},{12,14},{14,16},{16... | collective-permute-start | bytes 442376 | tf_op jit(solution)/shard_map/ppermute | solution.py:38
  21.1 13.6 %collective-permute-start.1 = (f32[36,8,128]{2,1,0:T(8,128)S(1)}, f32[36,8,128]{2,1,0:T(8,128)S(1)}, u32[]{:S(2)}, u32[]{:S(2)}) collective-permute-start(f32[36,8,128]{2,1,0:T(8,128)S(1)} %get-tuple-element.10), channel_id=1, source_target_pairs={{2,0},{4,2},{6,4},{8,6},{10,8},{12,10},{14,12},{16,14},{18,16},{20... | collective-permute-start | bytes 442376 | tf_op jit(solution)/shard_map/ppermute | solution.py:38

commit v2 on v1

v2 whole, which is shorter than its diff:
```python
import math

import jax
import jax.numpy as jnp
from jax import lax
from jax.experimental import pallas as pl
from jax.experimental.pallas import tpu as pltpu
from jax.sharding import PartitionSpec as P

SNAPS = 24
NH = 11
NV = 5
OWN = 12
OMEGA = 0.15
SUB, LANE = 8, 128
ROWS = NV * OWN
FIELD = 2 * ROWS
FACE_ROWS = 5 * OWN // 2
MPITCH = OWN * 32 + 8
CHUNKS = 2
CHUNK = OWN // CHUNKS
OUT_CHUNKS = 3
OUT_CHUNK = OWN // OUT_CHUNKS


def derivative_weights():
    weights = [0.0]
    for n in range(1, 12):
        total = sum(k * math.sin(2 * math.pi * ((k * n) % SNAPS) / SNAPS) for k in range(1, NH + 1))
        weights.append(-(2.0 / SNAPS) * total)
    return weights


DERIV = derivative_weights()


def exchanged(block, late):
    count, cores = lax.axis_size("blade"), lax.axis_size("inst")
    route = []
    for i in range(count):
        for core in range(cores):
            partner = (i + 1 if (i + core + late) % 2 == 1 else i - 1) % count
            route.append((i * cores + core, partner * cores + core))
    return lax.ppermute(block, ("blade", "inst"), route)


def first_face():
    return (lax.axis_index("blade") + lax.axis_index("inst") + 1) % 2


def lanes():
    return lax.broadcasted_iota(jnp.int32, (SUB, LANE), 1)


def sublanes():
    return lax.broadcasted_iota(jnp.int32, (SUB, LANE), 0)


def take(x, index):
    return jnp.take_along_axis(x, index, axis=1, mode="promise_in_bounds")


def quarters(row):
    first = jnp.broadcast_to(row[:, :LANE], (SUB, LANE))
    second = jnp.broadcast_to(row[:, LANE:], (SUB, LANE))
    sub = sublanes()
    both = jnp.where(sub < 4, first, second)
    return take(both, 32 * (sub & 3) + (lanes() & 31))


def wide(row):
    return jnp.concatenate([row[:, LANE * k : LANE * (k + 1)] for k in range(SUB)], axis=0)


def load_blocks(blocks, scratch, t):
    for k in range(SUB):
        tile = blocks[0, t, :, LANE * k : LANE * (k + 1)].astype(jnp.float32)
        scratch[pl.ds(pl.multiple_of(k * MPITCH + t * 32, 8), NV * NV), :] = tile


def fetch(pairs, sems):
    copies = [pltpu.make_async_copy(src, dst, sems.at[n]) for n, (src, dst) in enumerate(pairs)]
    for copy in copies:
        copy.start()
    return copies


def fetch_blocks(blocks, scratch, sems):
    return fetch(
        [(blocks.at[:, pl.ds(CHUNK * n, CHUNK)], scratch.at[:, pl.ds(CHUNK * n, CHUNK)]) for n in range(CHUNKS)],
        sems,
    )


def block_row(scratch, t, ij):
    return scratch[pl.ds(t * 32 + ij, SUB, stride=MPITCH), :]


def packed(parts, quarter):
    result = parts[-1]
    for g in reversed(range(len(parts) - 1)):
        result = jnp.where(quarter == g, parts[g], result)
    return result


def phase_weights(phase, rho):
    shape = (16, LANE)
    order = lax.broadcasted_iota(jnp.int32, shape, 0) + 1
    lag = lax.broadcasted_iota(jnp.int32, shape, 1)
    padded = jnp.concatenate([phase[...], jnp.zeros((1, LANE - NH), jnp.int32)], axis=1)
    spread = jnp.where(lag == order - 1, jnp.broadcast_to(padded, shape), 0).astype(jnp.float32)
    index = jnp.sum(spread, axis=1, keepdims=True)
    turns = (32 * order * (lag & 31)).astype(jnp.float32) - 3.0 * index
    turns = turns - 768.0 * jnp.floor(turns * (1.0 / 768.0) + 0.5)
    waves = jnp.where(order <= NH, jnp.cos(turns * (2.0 * math.pi / 768.0)), 0.0)
    parity = (1 - (lag[:1] & 1)).astype(jnp.float32)
    row = (2.0 / SNAPS) * (parity + jnp.sum(waves, axis=0, keepdims=True))
    for n in range(SNAPS):
        value = jnp.broadcast_to(row[:, n : n + 1], (SUB, LANE))
        rho[0, (-n) % SNAPS] = value
        rho[1, n] = value


def dual_kernel(
    phase, tangent, adjoint, precond, up_weight, lo_weight, up_cells, lo_cells,
    out, m_s, rho, index, scale, p_v, a_v, ph, uw, lw, uc, lc, t_sem, p_sem, w_sem,
):
    small = fetch(
        [(phase, ph), (up_weight, uw), (lo_weight, lw), (up_cells, uc), (lo_cells, lc)], w_sem
    )
    seeds = fetch([(adjoint, a_v), (tangent, out.at[pl.ds(0, ROWS)])], t_sem)
    chunks = fetch_blocks(precond, p_v, p_sem)
    for copy in small:
        copy.wait()
    phase_weights(ph, rho)
    index[0] = quarters(uc[...]) & (LANE - 1)
    index[1] = quarters(lc[...]) & (LANE - 1)
    up_scale = quarters(uw[...])
    lo_scale = quarters(lw[...])
    quarter = lanes() >> 5
    scale[0] = up_scale
    scale[1] = lo_scale
    scale[2] = jnp.where(quarter == 0, 1.0, up_scale)
    scale[3] = jnp.where(quarter == 1, 1.0, lo_scale)
    scale[4] = jnp.where(quarter == 0, lo_scale, 1.0)
    scale[5] = jnp.where(quarter == 1, up_scale, 1.0)

    def apply(t):
        seed = [a_v[i * OWN + t] for i in range(NV)]
        for j in range(NV):
            total = block_row(m_s, t, j) * seed[0]
            for i in range(1, NV):
                total = total + block_row(m_s, t, i * NV + j) * seed[i]
            out[ROWS + j * OWN + t] = total

    seeds[0].wait()
    for t in range(OWN):
        if t % CHUNK == 0:
            chunks[t // CHUNK].wait()
        load_blocks(p_v, m_s, t)
        if t > 0:
            apply(t - 1)
    apply(OWN - 1)
    seeds[1].wait()


def early():
    return lax.axis_index("blade") == 0


def local_work(gathered, jacobian, upwind, out, m_s, mix):
    own = lax.axis_index("inst")

    for fld, sign in ((0, 1.0), (1, -1.0)):

        def mix_body(i, carry):
            base = (fld * NV + i) * OWN
            mine = [gathered[own, base + s] for s in range(OWN)]
            theirs = [gathered[1 - own, base + s] for s in range(OWN)]
            ring = mine + theirs
            for r in range(OWN):
                total = None
                for k in range(1, OWN):
                    term = (sign * OMEGA * DERIV[k]) * (ring[(r - k) % SNAPS] - ring[(r + k) % SNAPS])
                    total = term if total is None else total + term
                mix[base + r] = total
            return carry

        lax.fori_loop(0, NV, mix_body, 0)

    lane = lanes()
    cell = sublanes() * LANE + lane
    flow = jnp.where(cell == 0, 0.0, wide(upwind[...]))

    def body(t, carry):
        tangent = [gathered[own, i * OWN + t] for i in range(NV)]
        dual = [gathered[own, (NV + i) * OWN + t] for i in range(NV)]
        sums = [None] * NV
        dsums = [None] * NV
        for i in range(NV):
            for j in range(NV):
                m = block_row(m_s, t, i * NV + j)
                term = m * tangent[j]
                sums[i] = term if j == 0 else sums[i] + term
                term = m * dual[i]
                dsums[j] = term if i == 0 else dsums[j] + term
        for i in range(NV):
            x = pltpu.roll(tangent[i], 1, 1)
            x = jnp.where(lane == 0, pltpu.roll(x, 1, 0), x)
            out[i * OWN + t] = sums[i] - flow * x + mix[i * OWN + t]
            x = pltpu.roll(flow * dual[i], LANE - 1, 1)
            x = jnp.where(lane == LANE - 1, pltpu.roll(x, SUB - 1, 0), x)
            out[(NV + i) * OWN + t] = dsums[i] - x + mix[(NV + i) * OWN + t]
        return carry

    def prepare(t, carry):
        load_blocks(jacobian, m_s, t)
        return carry

    lax.fori_loop(0, OWN, prepare, 0)
    lax.fori_loop(0, OWN, body, 0)


def local_kernel(gathered, jacobian, upwind, given, out, m_s, mix):
    @pl.when(jnp.logical_not(early()))
    def _():
        local_work(gathered, jacobian, upwind, out, m_s, mix)


def rotate_kernel(
    gathered, jacobian, upwind, rho, index, scale, ahead, after, partial, f_s, m_s, mix
):
    own = lax.axis_index("inst")
    first = first_face()
    quarter = lanes() >> 5
    odd = (quarter & 1) == 1
    even_rows = jnp.where(odd, index[1], index[0])
    odd_rows = jnp.where(odd, index[0], index[1])

    for n in range(SNAPS):
        core, t = (own, n) if n < OWN else (1 - own, n - OWN)
        rows = [
            take(gathered[core, q * OWN + t], odd_rows if q % 2 else even_rows)
            for q in range(2 * NV)
        ]
        for side in range(2):
            order = [rows[q ^ side] for q in range(2 * NV)]
            f_s[side, 0, n] = packed(order[:4], quarter)
            f_s[side, 1, n] = packed(order[4:8], quarter)
            f_s[side, 2, n] = jnp.where(odd, order[9], order[8])

    for result, which in ((ahead, first), (after, 1 - first)):
        for j in range(3):
            sums = [None] * OWN
            for s in range(SNAPS):
                x = f_s[which, j, s]
                for r in range(OWN):
                    term = rho[which, (r - s) % SNAPS] * x
                    sums[r] = term if sums[r] is None else sums[r] + term
            if j == 0:
                for r in range(OWN):
                    result[r] = sums[r]
            elif j == 1:
                for r in range(OWN):
                    result[OWN + r] = sums[r] * scale[2 + which]
            else:
                for r in range(OWN // 2):
                    both = jnp.where(quarter < 2, sums[r], sums[r + OWN // 2])
                    result[2 * OWN + r] = both * scale[which]

    @pl.when(early())
    def _():
        local_work(gathered, jacobian, upwind, partial, m_s, mix)


def final_kernel(
    partial, ahead, after, m_s, index, scale, tangent_out, adjoint_out, t_v, a_v, o_sem
):
    first = first_face()
    lane = lanes()
    group = lane >> 2
    faces = []
    for face, which in ((after, first), (ahead, 1 - first)):
        hit = take(index[1 - which], group) == lane
        spots = [group + 32 * (g + which * (1 - 2 * (g % 2))) for g in range(4)]
        faces.append((face, hit, spots, scale[1 - which], scale[4 + which]))

    def apply(t):
        half, low = divmod(t, OWN // 2)
        rows = [partial[q * OWN + t] for q in range(2 * NV)]
        for face, hit, spots, full, mid in faces:
            parts = [face[t] * full, face[OWN + t] * mid, face[2 * OWN + low]]
            for q in range(2 * NV):
                g = q % 4 + 2 * half if q >= 8 else q % 4
                rows[q] = rows[q] - jnp.where(hit, take(parts[q // 4], spots[g]), 0.0)
        for i in range(NV):
            total = block_row(m_s, t, i * NV) * rows[0]
            for j in range(1, NV):
                total = total + block_row(m_s, t, i * NV + j) * rows[j]
            t_v[i, t] = total
            a_v[i, t] = rows[NV + i]

    copies = []
    for n in range(OUT_CHUNKS):
        span = pl.ds(OUT_CHUNK * n, OUT_CHUNK)
        for t in range(OUT_CHUNK * n, OUT_CHUNK * (n + 1)):
            apply(t)
        for side, (src, dst) in enumerate(((t_v, tangent_out), (a_v, adjoint_out))):
            copy = pltpu.make_async_copy(src.at[:, span], dst.at[:, span], o_sem.at[2 * n + side])
            copy.start()
            copies.append(copy)
    for copy in copies:
        copy.wait()


def rows_of(count):
    return jax.ShapeDtypeStruct((count, SUB, LANE), jnp.float32)


BLOCK = (SUB * MPITCH, LANE)
BLOCKS = jax.ShapeDtypeStruct(BLOCK, jnp.float32)
HBM = pl.BlockSpec(memory_space=pltpu.HBM)
VMEM = pl.BlockSpec(memory_space=pltpu.VMEM)


def held(shape, dtype=jnp.float32):
    return pltpu.VMEM(shape, dtype)


def sems(count):
    return pltpu.SemaphoreType.DMA((count,))


def call(kernel, in_specs, out_shape, scratch, name, aliases={}, **kinds):
    return pl.pallas_call(
        kernel,
        in_specs=in_specs,
        out_shape=out_shape,
        scratch_shapes=scratch,
        input_output_aliases=aliases,
        compiler_params=pltpu.CompilerParams(vmem_limit_bytes=24 << 20),
        name=name,
        **kinds,
    )


def on_device(
    tangent_seed,
    adjoint_seed,
    jacobian,
    precond,
    upwind,
    up_weight,
    bottom_face_strength,
    up_cells,
    lo_cells,
    phase_index,
):
    face = up_cells.shape[0]
    tables = (phase_index.reshape(1, phase_index.shape[0]), up_weight, bottom_face_strength, up_cells.reshape(1, face), lo_cells.reshape(1, face))
    rows = (ROWS, SUB, LANE)
    both = (2, FIELD, SUB, LANE)
    fields, precond_rows, rho, index, scale = call(
        dual_kernel,
        [HBM] * 8,
        (
            rows_of(FIELD),
            BLOCKS,
            jax.ShapeDtypeStruct((2, SNAPS, SUB, LANE), jnp.float32),
            jax.ShapeDtypeStruct((2, SUB, LANE), jnp.int32),
            rows_of(6),
        ),
        [
            held(precond.shape, precond.dtype),
            held(rows),
            held(tables[0].shape, jnp.int32),
            held((1, face)),
            held((1, face)),
            held((1, face), jnp.int32),
            held((1, face), jnp.int32),
            sems(2),
            sems(CHUNKS),
            sems(5),
        ],
        "dual",
    )(
        *[
            pltpu.with_memory_space_constraint(x, pltpu.HBM)
            for x in (tables[0], tangent_seed.reshape(rows), adjoint_seed.reshape(rows), precond, *tables[1:])
        ],
    )
    gathered = lax.all_gather(fields, "inst", axis=0, tiled=True).reshape(both)
    local_scratch = [held(BLOCK), held((FIELD, SUB, LANE))]
    ahead, after, partial = call(
        rotate_kernel,
        [VMEM] * 6,
        (rows_of(FACE_ROWS), rows_of(FACE_ROWS), rows_of(FIELD)),
        [held((2, 3, SNAPS, SUB, LANE)), *local_scratch],
        "rotate",
    )(gathered, jacobian, upwind, rho, index, scale)
    ahead = exchanged(ahead, 0)
    after = exchanged(after, 1)
    partial = call(
        local_kernel, [VMEM] * 4, rows_of(FIELD), local_scratch, "local", {3: 0}
    )(gathered, jacobian, upwind, partial)
    out = (NV, OWN, SUB, LANE)
    tangent_out, adjoint_out = call(
        final_kernel,
        [VMEM] * 6,
        (jax.ShapeDtypeStruct(out, jnp.float32), jax.ShapeDtypeStruct(out, jnp.float32)),
        [held(out), held(out), sems(2 * OUT_CHUNKS)],
        "final",
        out_specs=(HBM, HBM),
    )(partial, ahead, after, precond_rows, index, scale)
    return tangent_out.reshape(tangent_seed.shape), adjoint_out.reshape(adjoint_seed.shape)


def solution(mesh):
    in_specs = (
        P("blade", None, "inst", None),
        P("blade", None, "inst", None),
        P("blade", "inst", None, None),
        P("blade", "inst", None, None),
        P("blade", None),
        P("blade", None),
        P("blade", None),
        P(),
        P(),
        P(),
    )
    out_specs = (P("blade", None, "inst", None), P("blade", None, "inst", None))
    return jax.shard_map(
        on_device, mesh=mesh, in_specs=in_specs, out_specs=out_specs, check_vma=False
    )
```

time: 37.3 us -> 28.9 us (0.77)
  Pallas kernels: 11.9 us -> 5.61 us
  local copies, waits for them, and re-layouts: 3.06 us -> 0.01 us
  waiting for transfers between devices: 0.01 us -> 2.22 us
  starting transfers between devices: 12.3 us -> 11.1 us
    pallas_call x4, Pallas kernels: 11.9 us -> 5.61 us  [the longest x1 2.45 us: on_device(): call(rotate_kernel, [VMEM] * 6, (rows_of(FACE_ROWS), rows_of(FACE_ROWS),...]
    unnamed x20 -> x4, local copies, waits for them, and re-layouts: 3.06 us -> 0.01 us
    ppermute x2, waiting for transfers between devices: 0.01 us -> 2.22 us  [exchanged(): return lax.ppermute(block, ('blade', 'inst'), route)]
    ppermute x2, starting transfers between devices: 12.3 us -> 11.1 us  [exchanged(): return lax.ppermute(block, ('blade', 'inst'), route)]
  transfers between devices with their start and end apart: 2 -> 2, of which waited for: 0 -> 1; matrix products, arithmetic and copies ran while one was open for 0% -> 0% of each run, Pallas kernels for 8% -> 0%
where the time goes in v2:
time: 28.9 us; the launch traced here: 28.7 us
  starting transfers between devices  11.1 us (38%)
  blocking collectives  9.01 us (31%)
  Pallas kernels  5.61 us (19%)
  waiting for transfers between devices  2.22 us (8%)
  between operations  0.7 us (2%)
    ppermute x2, starting transfers between devices, exchanged(): return lax.ppermute(block, ('blade', 'inst'), route)  11.1 us
    all_gather x1, blocking collectives, on_device(): gathered = lax.all_gather(fields, 'inst', axis=0, tiled=True).reshape(both)  9.01 us
    pallas_call x1, Pallas kernels, on_device(): call(rotate_kernel, [VMEM] * 6, (rows_of(FACE_ROWS), rows_of(FACE_ROWS),...  2.45 us
    ppermute x2, waiting for transfers between devices, exchanged(): return lax.ppermute(block, ('blade', 'inst'), route)  2.22 us
    pallas_call x1, Pallas kernels, on_device(): call(dual_kernel, [HBM] * 8, (rows_of(FIELD), BLOCKS, jax.ShapeDtypeStruc...  1.7 us
    pallas_call x1, Pallas kernels, on_device(): call(final_kernel, [VMEM] * 6, (jax.ShapeDtypeStruct(out, jnp.float32), j...  1.44 us
  transfers between devices with their start and end apart: 2, of which 1 were waited for; matrix products, arithmetic and copies ran while one was open for 0% of the time, Pallas kernels for 0%

profile of v2, /device:TPU:1, one launch (start us, length us, event | category | flops | bytes accessed | tf_op | source)
XLA Modules:
  0.0 28.7 jit_solution(6580452888536055457)
XLA Ops:
  0.6 0.0 copy-start.1
  0.6 0.0 copy-start
  0.7 1.7 %dual.1 = (f32[120,8,128]{2,1,0:T(8,128)S(1)}, f32[3136,128]{1,0:T(8,128)S(1)}, f32[2,24,8,128]{3,2,1,0:T(8,128)S(1)}, s32[2,8,128]{2,1,0:T(8,128)S(1)}, f32[6,8,128]{2,1,0:T(8,128)S(1)}) custom-call(s32[1,11]{1,0:T(1,128)} %bitcast.14, f32[60,8,128]{2,1,0:T(8,128)} %bitcast.10, f32[60,8,128]{2,1,0:T(8,128)} %bitcast.11, bf16[1,12,25,1024]{3,2,1,0:T(8,128)(2,1)} %precond.1, ...), custom_call_target="tpu_custom_call" | custom-call | tf_op jit(solution)/shard_map/dual/pallas_call | solution.py:363
  2.4 9.0 %all_gather.3 = f32[240,8,128]{2,1,0:T(8,128)S(1)} all-gather(f32[120,8,128]{2,1,0:T(8,128)S(1)} %get-tuple-element.12), channel_id=1, replica_groups=mesh['blade'=256,'inst'=2] {'inst'}, dimensions={0}, use_global_device_ids=true | all-gather | bytes 1474560 | tf_op jit(solution)/shard_map/all_gather | solution.py:392
  11.4 0.0 copy-done.1
  11.4 0.0 copy-done
  11.4 2.5 %rotate.1 = (f32[30,8,128]{2,1,0:T(8,128)S(1)}, f32[30,8,128]{2,1,0:T(8,128)S(1)}, f32[120,8,128]{2,1,0:T(8,128)S(1)}) custom-call(f32[2,120,8,128]{3,2,1,0:T(8,128)S(1)} %bitcast.8, bf16[1,12,25,1024]{3,2,1,0:T(8,128)(2,1)S(1)} %copy-done, f32[1,1024]{1,0:T(1,128)S(1)} %copy-done.1, f32[2,24,8,128]{3,2,1,0:T(8,128)S(1)} %get-tuple-element.13.rho, ...), custom_call_target="tpu_custom_call" | custom-call | tf_op jit(solution)/shard_map/rotate/pallas_call | solution.py:394
  13.8 1.9 %collective-permute-start = (f32[30,8,128]{2,1,0:T(8,128)S(1)}, f32[30,8,128]{2,1,0:T(8,128)S(1)}, u32[]{:S(2)}, u32[]{:S(2)}) collective-permute-start(f32[30,8,128]{2,1,0:T(8,128)S(1)} %get-tuple-element.17), channel_id=1, source_target_pairs={{0,510},{1,3},{2,4},{3,1},{4,2},{5,7},{6,8},{7,5},{8,6},{9,11},{10... | collective-permute-start | bytes 368648 | tf_op jit(solution)/shard_map/ppermute | solution.py:44
  15.8 9.2 %collective-permute-start.1 = (f32[30,8,128]{2,1,0:T(8,128)S(1)}, f32[30,8,128]{2,1,0:T(8,128)S(1)}, u32[]{:S(2)}, u32[]{:S(2)}) collective-permute-start(f32[30,8,128]{2,1,0:T(8,128)S(1)} %get-tuple-element.18), channel_id=1, source_target_pairs={{0,2},{1,511},{2,0},{3,5},{4,6},{5,3},{6,4},{7,9},{8,10},{9,7},{10... | collective-permute-start | bytes 368648 | tf_op jit(solution)/shard_map/ppermute | solution.py:44
  25.0 0.0 collective-permute-done.ahead
  25.0 2.2 %collective-permute-done.1.after = f32[30,8,128]{2,1,0:T(8,128)S(1)} collective-permute-done((f32[30,8,128]{2,1,0:T(8,128)S(1)}, f32[30,8,128]{2,1,0:T(8,128)S(1)}, u32[]{:S(2)}, u32[]{:S(2)}) %collective-permute-start.1) | collective-permute-done | bytes 122912 | tf_op jit(solution)/shard_map/ppermute | solution.py:44
  27.2 1.4 %final.1 = (f32[5,12,8,128]{3,2,1,0:T(8,128)}, f32[5,12,8,128]{3,2,1,0:T(8,128)}) custom-call(f32[120,8,128]{2,1,0:T(8,128)S(1)} %local.1.partial, f32[30,8,128]{2,1,0:T(8,128)S(1)} %collective-permute-done.ahead, f32[30,8,128]{2,1,0:T(8,128)S(1)} %collective-permute-done.1.after, f32[3136,128]{1,0:T(8,128)S(1)} %get-tuple-element.19.m_s, ...), custom_call_target="tpu_custom_call" | custom-call | tf_op jit(solution)/shard_map/final/pallas_call | solution.py:407
  (1 shorter events, 0.0 us)
Async XLA Ops:
  0.6 10.7 %copy-start.1 = (f32[1,1024]{1,0:T(1,128)S(1)}, f32[1,1024]{1,0:T(1,128)}, u32[]{:S(2)}) copy-start(f32[1,1024]{1,0:T(1,128)} %upwind.3) | copy-start | bytes 12292
  0.6 10.7 %copy-start = (bf16[1,12,25,1024]{3,2,1,0:T(8,128)(2,1)S(1)}, bf16[1,12,25,1024]{3,2,1,0:T(8,128)(2,1)}, u32[]{:S(2)}) copy-start(bf16[1,12,25,1024]{3,2,1,0:T(8,128)(2,1)} %jacobian.3) | copy-start | bytes 1843204
  13.8 11.2 %collective-permute-start = (f32[30,8,128]{2,1,0:T(8,128)S(1)}, f32[30,8,128]{2,1,0:T(8,128)S(1)}, u32[]{:S(2)}, u32[]{:S(2)}) collective-permute-start(f32[30,8,128]{2,1,0:T(8,128)S(1)} %get-tuple-element.17), channel_id=1, source_target_pairs={{0,510},{1,3},{2,4},{3,1},{4,2},{5,7},{6,8},{7,5},{8,6},{9,11},{10... | collective-permute-start | bytes 368648 | tf_op jit(solution)/shard_map/ppermute | solution.py:44
  15.8 11.5 %collective-permute-start.1 = (f32[30,8,128]{2,1,0:T(8,128)S(1)}, f32[30,8,128]{2,1,0:T(8,128)S(1)}, u32[]{:S(2)}, u32[]{:S(2)}) collective-permute-start(f32[30,8,128]{2,1,0:T(8,128)S(1)} %get-tuple-element.18), channel_id=1, source_target_pairs={{0,2},{1,511},{2,0},{3,5},{4,6},{5,3},{6,4},{7,9},{8,10},{9,7},{10... | collective-permute-start | bytes 368648 | tf_op jit(solution)/shard_map/ppermute | solution.py:44

commit v3 on v2

--- a/solution.py
+++ b/solution.py
@@ -221,10 +221,33 @@
     lax.fori_loop(0, OWN, body, 0)
 
 
-def local_kernel(gathered, jacobian, upwind, given, out, m_s, mix):
+def received(face, which, index, scale):
+    lane = lanes()
+    group = lane >> 2
+    hit = take(index[1 - which], group) == lane
+    spots = [group + 32 * (g + which * (1 - 2 * (g % 2))) for g in range(4)]
+    full, mid = scale[1 - which], scale[4 + which]
+
+    def terms(t):
+        half, low = divmod(t, OWN // 2)
+        parts = [face[t] * full, face[OWN + t] * mid, face[2 * OWN + low]]
+        return [
+            jnp.where(hit, take(parts[q // 4], spots[q % 4 + (2 * half if q >= 8 else 0)]), 0.0)
+            for q in range(2 * NV)
+        ]
+
+    return terms
+
+
+def local_kernel(gathered, jacobian, upwind, given, ahead, index, scale, out, m_s, mix):
     @pl.when(jnp.logical_not(early()))
     def _():
         local_work(gathered, jacobian, upwind, out, m_s, mix)
+
+    terms = received(ahead, 1 - first_face(), index, scale)
+    for t in range(OWN):
+        for q, term in enumerate(terms(t)):
+            out[q * OWN + t] = out[q * OWN + t] - term
 
 
 def rotate_kernel(
@@ -274,25 +297,12 @@
 
 
 def final_kernel(
-    partial, ahead, after, m_s, index, scale, tangent_out, adjoint_out, t_v, a_v, o_sem
+    partial, after, m_s, index, scale, tangent_out, adjoint_out, t_v, a_v, o_sem
 ):
-    first = first_face()
-    lane = lanes()
-    group = lane >> 2
-    faces = []
-    for face, which in ((after, first), (ahead, 1 - first)):
-        hit = take(index[1 - which], group) == lane
-        spots = [group + 32 * (g + which * (1 - 2 * (g % 2))) for g in range(4)]
-        faces.append((face, hit, spots, scale[1 - which], scale[4 + which]))
+    terms = received(after, first_face(), index, scale)
 
     def apply(t):
-        half, low = divmod(t, OWN // 2)
-        rows = [partial[q * OWN + t] for q in range(2 * NV)]
-        for face, hit, spots, full, mid in faces:
-            parts = [face[t] * full, face[OWN + t] * mid, face[2 * OWN + low]]
-            for q in range(2 * NV):
-                g = q % 4 + 2 * half if q >= 8 else q % 4
-                rows[q] = rows[q] - jnp.where(hit, take(parts[q // 4], spots[g]), 0.0)
+        rows = [partial[q * OWN + t] - term for q, term in enumerate(terms(t))]
         for i in range(NV):
             total = block_row(m_s, t, i * NV) * rows[0]
             for j in range(1, NV):
@@ -401,17 +411,17 @@
     ahead = exchanged(ahead, 0)
     after = exchanged(after, 1)
     partial = call(
-        local_kernel, [VMEM] * 4, rows_of(FIELD), local_scratch, "local", {3: 0}
-    )(gathered, jacobian, upwind, partial)
+        local_kernel, [VMEM] * 7, rows_of(FIELD), local_scratch, "local", {3: 0}
+    )(gathered, jacobian, upwind, partial, ahead, index, scale)
     out = (NV, OWN, SUB, LANE)
     tangent_out, adjoint_out = call(
         final_kernel,
-        [VMEM] * 6,
+        [VMEM] * 5,
         (jax.ShapeDtypeStruct(out, jnp.float32), jax.ShapeDtypeStruct(out, jnp.float32)),
         [held(out), held(out), sems(2 * OUT_CHUNKS)],
         "final",
         out_specs=(HBM, HBM),
-    )(partial, ahead, after, precond_rows, index, scale)
+    )(partial, after, precond_rows, index, scale)
     return tangent_out.reshape(tangent_seed.shape), adjoint_out.reshape(adjoint_seed.shape)
 
 

time: 28.9 us -> 28.5 us (0.986)
  waiting for transfers between devices: 2.22 us -> 1.84 us
    ppermute x2, waiting for transfers between devices: 2.22 us -> 1.84 us  [exchanged(): return lax.ppermute(block, ('blade', 'inst'), route)]
  transfers between devices with their start and end apart: 2 -> 2, of which waited for: 1 -> 1; matrix products, arithmetic and copies ran while one was open for 0% -> 0% of each run, Pallas kernels for 0% -> 1%
where the time goes in v3:
time: 28.5 us; the launch traced here: 28.3 us
  starting transfers between devices  11.1 us (39%)
  blocking collectives  9.01 us (32%)
  Pallas kernels  5.65 us (20%)
  waiting for transfers between devices  1.84 us (6%)
  between operations  0.69 us (2%)
    ppermute x2, starting transfers between devices, exchanged(): return lax.ppermute(block, ('blade', 'inst'), route)  11.1 us
    all_gather x1, blocking collectives, on_device(): gathered = lax.all_gather(fields, 'inst', axis=0, tiled=True).reshape(both)  9.01 us
    pallas_call x1, Pallas kernels, on_device(): call(rotate_kernel, [VMEM] * 6, (rows_of(FACE_ROWS), rows_of(FACE_ROWS),...  2.45 us
    ppermute x2, waiting for transfers between devices, exchanged(): return lax.ppermute(block, ('blade', 'inst'), route)  1.84 us
    pallas_call x1, Pallas kernels, on_device(): call(dual_kernel, [HBM] * 8, (rows_of(FIELD), BLOCKS, jax.ShapeDtypeStruc...  1.7 us
    pallas_call x1, Pallas kernels, on_device(): call(final_kernel, [VMEM] * 5, (jax.ShapeDtypeStruct(out, jnp.float32), j...  1.1 us
  transfers between devices with their start and end apart: 2, of which 1 were waited for; matrix products, arithmetic and copies ran while one was open for 0% of the time, Pallas kernels for 1%

profile of v3, /device:TPU:1, one launch (start us, length us, event | category | flops | bytes accessed | tf_op | source)
XLA Modules:
  0.0 28.3 jit_solution(15254707349843583775)
XLA Ops:
  0.6 0.0 copy-start.1
  0.6 0.0 copy-start
  0.7 1.7 %dual.1 = (f32[120,8,128]{2,1,0:T(8,128)S(1)}, f32[3136,128]{1,0:T(8,128)S(1)}, f32[2,24,8,128]{3,2,1,0:T(8,128)S(1)}, s32[2,8,128]{2,1,0:T(8,128)S(1)}, f32[6,8,128]{2,1,0:T(8,128)S(1)}) custom-call(s32[1,11]{1,0:T(1,128)} %bitcast.14, f32[60,8,128]{2,1,0:T(8,128)} %bitcast.10, f32[60,8,128]{2,1,0:T(8,128)} %bitcast.11, bf16[1,12,25,1024]{3,2,1,0:T(8,128)(2,1)} %precond.1, ...), custom_call_target="tpu_custom_call" | custom-call | tf_op jit(solution)/shard_map/dual/pallas_call | solution.py:373
  2.4 9.0 %all_gather.3 = f32[240,8,128]{2,1,0:T(8,128)S(1)} all-gather(f32[120,8,128]{2,1,0:T(8,128)S(1)} %get-tuple-element.12), channel_id=1, replica_groups=mesh['blade'=256,'inst'=2] {'inst'}, dimensions={0}, use_global_device_ids=true | all-gather | bytes 1474560 | tf_op jit(solution)/shard_map/all_gather | solution.py:402
  11.4 0.0 copy-done.1
  11.4 0.0 copy-done
  11.4 2.4 %rotate.1 = (f32[30,8,128]{2,1,0:T(8,128)S(1)}, f32[30,8,128]{2,1,0:T(8,128)S(1)}, f32[120,8,128]{2,1,0:T(8,128)S(1)}) custom-call(f32[2,120,8,128]{3,2,1,0:T(8,128)S(1)} %bitcast.8, bf16[1,12,25,1024]{3,2,1,0:T(8,128)(2,1)S(1)} %copy-done, f32[1,1024]{1,0:T(1,128)S(1)} %copy-done.1, f32[2,24,8,128]{3,2,1,0:T(8,128)S(1)} %get-tuple-element.13.rho, ...), custom_call_target="tpu_custom_call" | custom-call | tf_op jit(solution)/shard_map/rotate/pallas_call | solution.py:404
  13.8 1.9 %collective-permute-start = (f32[30,8,128]{2,1,0:T(8,128)S(1)}, f32[30,8,128]{2,1,0:T(8,128)S(1)}, u32[]{:S(2)}, u32[]{:S(2)}) collective-permute-start(f32[30,8,128]{2,1,0:T(8,128)S(1)} %get-tuple-element.17), channel_id=1, source_target_pairs={{0,510},{1,3},{2,4},{3,1},{4,2},{5,7},{6,8},{7,5},{8,6},{9,11},{10... | collective-permute-start | bytes 368648 | tf_op jit(solution)/shard_map/ppermute | solution.py:44
  15.8 9.2 %collective-permute-start.1 = (f32[30,8,128]{2,1,0:T(8,128)S(1)}, f32[30,8,128]{2,1,0:T(8,128)S(1)}, u32[]{:S(2)}, u32[]{:S(2)}) collective-permute-start(f32[30,8,128]{2,1,0:T(8,128)S(1)} %get-tuple-element.18), channel_id=1, source_target_pairs={{0,2},{1,511},{2,0},{3,5},{4,6},{5,3},{6,4},{7,9},{8,10},{9,7},{10... | collective-permute-start | bytes 368648 | tf_op jit(solution)/shard_map/ppermute | solution.py:44
  25.0 0.0 collective-permute-done.ahead
  25.0 0.4 %local.1.partial = f32[120,8,128]{2,1,0:T(8,128)S(1)} custom-call(f32[2,120,8,128]{3,2,1,0:T(8,128)S(1)} %bitcast.9, bf16[1,12,25,1024]{3,2,1,0:T(8,128)(2,1)S(1)} %copy-done, f32[1,1024]{1,0:T(1,128)S(1)} %copy-done.1, f32[120,8,128]{2,1,0:T(8,128)S(1)} %get-tuple-element.16.given, ...), custom_call_target="tpu_custom_call", output_to_operand_aliasing={{}: (3, {})} | custom-call | tf_op jit(solution)/shard_map/local/pallas_call | solution.py:413
  25.4 1.8 %collective-permute-done.1.after = f32[30,8,128]{2,1,0:T(8,128)S(1)} collective-permute-done((f32[30,8,128]{2,1,0:T(8,128)S(1)}, f32[30,8,128]{2,1,0:T(8,128)S(1)}, u32[]{:S(2)}, u32[]{:S(2)}) %collective-permute-start.1) | collective-permute-done | bytes 122912 | tf_op jit(solution)/shard_map/ppermute | solution.py:44
  27.2 1.1 %final.1 = (f32[5,12,8,128]{3,2,1,0:T(8,128)}, f32[5,12,8,128]{3,2,1,0:T(8,128)}) custom-call(f32[120,8,128]{2,1,0:T(8,128)S(1)} %local.1.partial, f32[30,8,128]{2,1,0:T(8,128)S(1)} %collective-permute-done.1.after, f32[3136,128]{1,0:T(8,128)S(1)} %get-tuple-element.19.m_s, s32[2,8,128]{2,1,0:T(8,128)S(1)} %get-tuple-element.14.index, ...), custom_call_target="tpu_custom_call" | custom-call | tf_op jit(solution)/shard_map/final/pallas_call | solution.py:417
Async XLA Ops:
  0.6 10.7 %copy-start.1 = (f32[1,1024]{1,0:T(1,128)S(1)}, f32[1,1024]{1,0:T(1,128)}, u32[]{:S(2)}) copy-start(f32[1,1024]{1,0:T(1,128)} %upwind.3) | copy-start | bytes 12292
  0.6 10.7 %copy-start = (bf16[1,12,25,1024]{3,2,1,0:T(8,128)(2,1)S(1)}, bf16[1,12,25,1024]{3,2,1,0:T(8,128)(2,1)}, u32[]{:S(2)}) copy-start(bf16[1,12,25,1024]{3,2,1,0:T(8,128)(2,1)} %jacobian.3) | copy-start | bytes 1843204
  13.8 11.2 %collective-permute-start = (f32[30,8,128]{2,1,0:T(8,128)S(1)}, f32[30,8,128]{2,1,0:T(8,128)S(1)}, u32[]{:S(2)}, u32[]{:S(2)}) collective-permute-start(f32[30,8,128]{2,1,0:T(8,128)S(1)} %get-tuple-element.17), channel_id=1, source_target_pairs={{0,510},{1,3},{2,4},{3,1},{4,2},{5,7},{6,8},{7,5},{8,6},{9,11},{10... | collective-permute-start | bytes 368648 | tf_op jit(solution)/shard_map/ppermute | solution.py:44
  15.8 11.5 %collective-permute-start.1 = (f32[30,8,128]{2,1,0:T(8,128)S(1)}, f32[30,8,128]{2,1,0:T(8,128)S(1)}, u32[]{:S(2)}, u32[]{:S(2)}) collective-permute-start(f32[30,8,128]{2,1,0:T(8,128)S(1)} %get-tuple-element.18), channel_id=1, source_target_pairs={{0,2},{1,511},{2,0},{3,5},{4,6},{5,3},{6,4},{7,9},{8,10},{9,7},{10... | collective-permute-start | bytes 368648 | tf_op jit(solution)/shard_map/ppermute | solution.py:44

commit v4 on v3

--- a/solution.py
+++ b/solution.py
@@ -165,7 +165,7 @@
 
 
 def early():
-    return lax.axis_index("blade") == 0
+    return lax.axis_index("blade") < 2
 
 
 def local_work(gathered, jacobian, upwind, out, m_s, mix):

time: 28.5 us -> 28.5 us (level)
  no operation moved by 1% of the time
where the time goes in v4:
time: 28.5 us; the launch traced here: 28.3 us
  starting transfers between devices  11.1 us (39%)
  blocking collectives  9.01 us (32%)
  Pallas kernels  5.65 us (20%)
  waiting for transfers between devices  1.84 us (6%)
  between operations  0.69 us (2%)
    ppermute x2, starting transfers between devices, exchanged(): return lax.ppermute(block, ('blade', 'inst'), route)  11.1 us
    all_gather x1, blocking collectives, on_device(): gathered = lax.all_gather(fields, 'inst', axis=0, tiled=True).reshape(both)  9.01 us
    pallas_call x1, Pallas kernels, on_device(): call(rotate_kernel, [VMEM] * 6, (rows_of(FACE_ROWS), rows_of(FACE_ROWS),...  2.45 us
    ppermute x2, waiting for transfers between devices, exchanged(): return lax.ppermute(block, ('blade', 'inst'), route)  1.84 us
    pallas_call x1, Pallas kernels, on_device(): call(dual_kernel, [HBM] * 8, (rows_of(FIELD), BLOCKS, jax.ShapeDtypeStruc...  1.7 us
    pallas_call x1, Pallas kernels, on_device(): call(final_kernel, [VMEM] * 5, (jax.ShapeDtypeStruct(out, jnp.float32), j...  1.1 us
  transfers between devices with their start and end apart: 2, of which 1 were waited for; matrix products, arithmetic and copies ran while one was open for 0% of the time, Pallas kernels for 1%

profile of v4, /device:TPU:1, one launch (start us, length us, event | category | flops | bytes accessed | tf_op | source)
XLA Modules:
  0.0 28.3 jit_solution(6023618263354927326)
XLA Ops:
  0.6 0.0 copy-start.1
  0.6 0.0 copy-start
  0.7 1.7 %dual.1 = (f32[120,8,128]{2,1,0:T(8,128)S(1)}, f32[3136,128]{1,0:T(8,128)S(1)}, f32[2,24,8,128]{3,2,1,0:T(8,128)S(1)}, s32[2,8,128]{2,1,0:T(8,128)S(1)}, f32[6,8,128]{2,1,0:T(8,128)S(1)}) custom-call(s32[1,11]{1,0:T(1,128)} %bitcast.14, f32[60,8,128]{2,1,0:T(8,128)} %bitcast.10, f32[60,8,128]{2,1,0:T(8,128)} %bitcast.11, bf16[1,12,25,1024]{3,2,1,0:T(8,128)(2,1)} %precond.1, ...), custom_call_target="tpu_custom_call" | custom-call | tf_op jit(solution)/shard_map/dual/pallas_call | solution.py:373
  2.4 9.0 %all_gather.3 = f32[240,8,128]{2,1,0:T(8,128)S(1)} all-gather(f32[120,8,128]{2,1,0:T(8,128)S(1)} %get-tuple-element.12), channel_id=1, replica_groups=mesh['blade'=256,'inst'=2] {'inst'}, dimensions={0}, use_global_device_ids=true | all-gather | bytes 1474560 | tf_op jit(solution)/shard_map/all_gather | solution.py:402
  11.4 0.0 copy-done.1
  11.4 0.0 copy-done
  11.4 2.4 %rotate.1 = (f32[30,8,128]{2,1,0:T(8,128)S(1)}, f32[30,8,128]{2,1,0:T(8,128)S(1)}, f32[120,8,128]{2,1,0:T(8,128)S(1)}) custom-call(f32[2,120,8,128]{3,2,1,0:T(8,128)S(1)} %bitcast.8, bf16[1,12,25,1024]{3,2,1,0:T(8,128)(2,1)S(1)} %copy-done, f32[1,1024]{1,0:T(1,128)S(1)} %copy-done.1, f32[2,24,8,128]{3,2,1,0:T(8,128)S(1)} %get-tuple-element.13.rho, ...), custom_call_target="tpu_custom_call" | custom-call | tf_op jit(solution)/shard_map/rotate/pallas_call | solution.py:404
  13.8 1.9 %collective-permute-start = (f32[30,8,128]{2,1,0:T(8,128)S(1)}, f32[30,8,128]{2,1,0:T(8,128)S(1)}, u32[]{:S(2)}, u32[]{:S(2)}) collective-permute-start(f32[30,8,128]{2,1,0:T(8,128)S(1)} %get-tuple-element.17), channel_id=1, source_target_pairs={{0,510},{1,3},{2,4},{3,1},{4,2},{5,7},{6,8},{7,5},{8,6},{9,11},{10... | collective-permute-start | bytes 368648 | tf_op jit(solution)/shard_map/ppermute | solution.py:44
  15.8 9.2 %collective-permute-start.1 = (f32[30,8,128]{2,1,0:T(8,128)S(1)}, f32[30,8,128]{2,1,0:T(8,128)S(1)}, u32[]{:S(2)}, u32[]{:S(2)}) collective-permute-start(f32[30,8,128]{2,1,0:T(8,128)S(1)} %get-tuple-element.18), channel_id=1, source_target_pairs={{0,2},{1,511},{2,0},{3,5},{4,6},{5,3},{6,4},{7,9},{8,10},{9,7},{10... | collective-permute-start | bytes 368648 | tf_op jit(solution)/shard_map/ppermute | solution.py:44
  25.0 0.0 collective-permute-done.ahead
  25.0 0.4 %local.1.partial = f32[120,8,128]{2,1,0:T(8,128)S(1)} custom-call(f32[2,120,8,128]{3,2,1,0:T(8,128)S(1)} %bitcast.9, bf16[1,12,25,1024]{3,2,1,0:T(8,128)(2,1)S(1)} %copy-done, f32[1,1024]{1,0:T(1,128)S(1)} %copy-done.1, f32[120,8,128]{2,1,0:T(8,128)S(1)} %get-tuple-element.16.given, ...), custom_call_target="tpu_custom_call", output_to_operand_aliasing={{}: (3, {})} | custom-call | tf_op jit(solution)/shard_map/local/pallas_call | solution.py:413
  25.4 1.8 %collective-permute-done.1.after = f32[30,8,128]{2,1,0:T(8,128)S(1)} collective-permute-done((f32[30,8,128]{2,1,0:T(8,128)S(1)}, f32[30,8,128]{2,1,0:T(8,128)S(1)}, u32[]{:S(2)}, u32[]{:S(2)}) %collective-permute-start.1) | collective-permute-done | bytes 122912 | tf_op jit(solution)/shard_map/ppermute | solution.py:44
  27.2 1.1 %final.1 = (f32[5,12,8,128]{3,2,1,0:T(8,128)}, f32[5,12,8,128]{3,2,1,0:T(8,128)}) custom-call(f32[120,8,128]{2,1,0:T(8,128)S(1)} %local.1.partial, f32[30,8,128]{2,1,0:T(8,128)S(1)} %collective-permute-done.1.after, f32[3136,128]{1,0:T(8,128)S(1)} %get-tuple-element.19.m_s, s32[2,8,128]{2,1,0:T(8,128)S(1)} %get-tuple-element.14.index, ...), custom_call_target="tpu_custom_call" | custom-call | tf_op jit(solution)/shard_map/final/pallas_call | solution.py:417
Async XLA Ops:
  0.6 10.7 %copy-start.1 = (f32[1,1024]{1,0:T(1,128)S(1)}, f32[1,1024]{1,0:T(1,128)}, u32[]{:S(2)}) copy-start(f32[1,1024]{1,0:T(1,128)} %upwind.3) | copy-start | bytes 12292
  0.6 10.7 %copy-start = (bf16[1,12,25,1024]{3,2,1,0:T(8,128)(2,1)S(1)}, bf16[1,12,25,1024]{3,2,1,0:T(8,128)(2,1)}, u32[]{:S(2)}) copy-start(bf16[1,12,25,1024]{3,2,1,0:T(8,128)(2,1)} %jacobian.3) | copy-start | bytes 1843204
  13.8 11.2 %collective-permute-start = (f32[30,8,128]{2,1,0:T(8,128)S(1)}, f32[30,8,128]{2,1,0:T(8,128)S(1)}, u32[]{:S(2)}, u32[]{:S(2)}) collective-permute-start(f32[30,8,128]{2,1,0:T(8,128)S(1)} %get-tuple-element.17), channel_id=1, source_target_pairs={{0,510},{1,3},{2,4},{3,1},{4,2},{5,7},{6,8},{7,5},{8,6},{9,11},{10... | collective-permute-start | bytes 368648 | tf_op jit(solution)/shard_map/ppermute | solution.py:44
  15.8 11.5 %collective-permute-start.1 = (f32[30,8,128]{2,1,0:T(8,128)S(1)}, f32[30,8,128]{2,1,0:T(8,128)S(1)}, u32[]{:S(2)}, u32[]{:S(2)}) collective-permute-start(f32[30,8,128]{2,1,0:T(8,128)S(1)} %get-tuple-element.18), channel_id=1, source_target_pairs={{0,2},{1,511},{2,0},{3,5},{4,6},{5,3},{6,4},{7,9},{8,10},{9,7},{10... | collective-permute-start | bytes 368648 | tf_op jit(solution)/shard_map/ppermute | solution.py:44

commit v5 on v4

--- a/solution.py
+++ b/solution.py
@@ -39,13 +39,13 @@
     route = []
     for i in range(count):
         for core in range(cores):
-            partner = (i + 1 if (i + core + late) % 2 == 1 else i - 1) % count
+            partner = (i + 1 if (i + late) % 2 == 0 else i - 1) % count
             route.append((i * cores + core, partner * cores + core))
     return lax.ppermute(block, ("blade", "inst"), route)
 
 
 def first_face():
-    return (lax.axis_index("blade") + lax.axis_index("inst") + 1) % 2
+    return lax.axis_index("blade") % 2
 
 
 def lanes():

time: 28.5 us -> 29.3 us (1.028)
  waiting for transfers between devices: 1.84 us -> 2.65 us
    ppermute x2, waiting for transfers between devices: 1.84 us -> 2.65 us  [exchanged(): return lax.ppermute(block, ('blade', 'inst'), route)]
where the time goes in v5:
time: 29.3 us; the launch traced here: 29.1 us
  starting transfers between devices  11.1 us (38%)
  blocking collectives  9.01 us (31%)
  Pallas kernels  5.65 us (19%)
  waiting for transfers between devices  2.65 us (9%)
  between operations  0.69 us (2%)
    ppermute x2, starting transfers between devices, exchanged(): return lax.ppermute(block, ('blade', 'inst'), route)  11.1 us
    all_gather x1, blocking collectives, on_device(): gathered = lax.all_gather(fields, 'inst', axis=0, tiled=True).reshape(both)  9.01 us
    ppermute x2, waiting for transfers between devices, exchanged(): return lax.ppermute(block, ('blade', 'inst'), route)  2.65 us
    pallas_call x1, Pallas kernels, on_device(): call(rotate_kernel, [VMEM] * 6, (rows_of(FACE_ROWS), rows_of(FACE_ROWS),...  2.45 us
    pallas_call x1, Pallas kernels, on_device(): call(dual_kernel, [HBM] * 8, (rows_of(FIELD), BLOCKS, jax.ShapeDtypeStruc...  1.7 us
    pallas_call x1, Pallas kernels, on_device(): call(final_kernel, [VMEM] * 5, (jax.ShapeDtypeStruct(out, jnp.float32), j...  1.1 us
  transfers between devices with their start and end apart: 2, of which 1 were waited for; matrix products, arithmetic and copies ran while one was open for 0% of the time, Pallas kernels for 1%

profile of v5, /device:TPU:1, one launch (start us, length us, event | category | flops | bytes accessed | tf_op | source)
XLA Modules:
  0.0 29.1 jit_solution(2500806966727874505)
XLA Ops:
  0.6 0.0 copy-start.1
  0.6 0.0 copy-start
  0.7 1.7 %dual.1 = (f32[120,8,128]{2,1,0:T(8,128)S(1)}, f32[3136,128]{1,0:T(8,128)S(1)}, f32[2,24,8,128]{3,2,1,0:T(8,128)S(1)}, s32[2,8,128]{2,1,0:T(8,128)S(1)}, f32[6,8,128]{2,1,0:T(8,128)S(1)}) custom-call(s32[1,11]{1,0:T(1,128)} %bitcast.14, f32[60,8,128]{2,1,0:T(8,128)} %bitcast.10, f32[60,8,128]{2,1,0:T(8,128)} %bitcast.11, bf16[1,12,25,1024]{3,2,1,0:T(8,128)(2,1)} %precond.1, ...), custom_call_target="tpu_custom_call" | custom-call | tf_op jit(solution)/shard_map/dual/pallas_call | solution.py:373
  2.4 9.0 %all_gather.3 = f32[240,8,128]{2,1,0:T(8,128)S(1)} all-gather(f32[120,8,128]{2,1,0:T(8,128)S(1)} %get-tuple-element.12), channel_id=1, replica_groups=mesh['blade'=256,'inst'=2] {'inst'}, dimensions={0}, use_global_device_ids=true | all-gather | bytes 1474560 | tf_op jit(solution)/shard_map/all_gather | solution.py:402
  11.4 0.0 copy-done.1
  11.4 0.0 copy-done
  11.4 2.4 %rotate.1 = (f32[30,8,128]{2,1,0:T(8,128)S(1)}, f32[30,8,128]{2,1,0:T(8,128)S(1)}, f32[120,8,128]{2,1,0:T(8,128)S(1)}) custom-call(f32[2,120,8,128]{3,2,1,0:T(8,128)S(1)} %bitcast.8, bf16[1,12,25,1024]{3,2,1,0:T(8,128)(2,1)S(1)} %copy-done, f32[1,1024]{1,0:T(1,128)S(1)} %copy-done.1, f32[2,24,8,128]{3,2,1,0:T(8,128)S(1)} %get-tuple-element.13.rho, ...), custom_call_target="tpu_custom_call" | custom-call | tf_op jit(solution)/shard_map/rotate/pallas_call | solution.py:404
  13.8 1.9 %collective-permute-start = (f32[30,8,128]{2,1,0:T(8,128)S(1)}, f32[30,8,128]{2,1,0:T(8,128)S(1)}, u32[]{:S(2)}, u32[]{:S(2)}) collective-permute-start(f32[30,8,128]{2,1,0:T(8,128)S(1)} %get-tuple-element.17), channel_id=1, source_target_pairs={{0,2},{1,3},{2,0},{3,1},{4,6},{5,7},{6,4},{7,5},{8,10},{9,11},{10,... | collective-permute-start | bytes 368648 | tf_op jit(solution)/shard_map/ppermute | solution.py:44
  15.8 9.2 %collective-permute-start.1 = (f32[30,8,128]{2,1,0:T(8,128)S(1)}, f32[30,8,128]{2,1,0:T(8,128)S(1)}, u32[]{:S(2)}, u32[]{:S(2)}) collective-permute-start(f32[30,8,128]{2,1,0:T(8,128)S(1)} %get-tuple-element.18), channel_id=1, source_target_pairs={{0,510},{1,511},{2,4},{3,5},{4,2},{5,3},{6,8},{7,9},{8,6},{9,7},{1... | collective-permute-start | bytes 368648 | tf_op jit(solution)/shard_map/ppermute | solution.py:44
  25.0 0.0 collective-permute-done.ahead
  25.0 0.4 %local.1.partial = f32[120,8,128]{2,1,0:T(8,128)S(1)} custom-call(f32[2,120,8,128]{3,2,1,0:T(8,128)S(1)} %bitcast.9, bf16[1,12,25,1024]{3,2,1,0:T(8,128)(2,1)S(1)} %copy-done, f32[1,1024]{1,0:T(1,128)S(1)} %copy-done.1, f32[120,8,128]{2,1,0:T(8,128)S(1)} %get-tuple-element.16.given, ...), custom_call_target="tpu_custom_call", output_to_operand_aliasing={{}: (3, {})} | custom-call | tf_op jit(solution)/shard_map/local/pallas_call | solution.py:413
  25.4 2.6 %collective-permute-done.1.after = f32[30,8,128]{2,1,0:T(8,128)S(1)} collective-permute-done((f32[30,8,128]{2,1,0:T(8,128)S(1)}, f32[30,8,128]{2,1,0:T(8,128)S(1)}, u32[]{:S(2)}, u32[]{:S(2)}) %collective-permute-start.1) | collective-permute-done | bytes 122912 | tf_op jit(solution)/shard_map/ppermute | solution.py:44
  28.1 1.1 %final.1 = (f32[5,12,8,128]{3,2,1,0:T(8,128)}, f32[5,12,8,128]{3,2,1,0:T(8,128)}) custom-call(f32[120,8,128]{2,1,0:T(8,128)S(1)} %local.1.partial, f32[30,8,128]{2,1,0:T(8,128)S(1)} %collective-permute-done.1.after, f32[3136,128]{1,0:T(8,128)S(1)} %get-tuple-element.19.m_s, s32[2,8,128]{2,1,0:T(8,128)S(1)} %get-tuple-element.14.index, ...), custom_call_target="tpu_custom_call" | custom-call | tf_op jit(solution)/shard_map/final/pallas_call | solution.py:417
Async XLA Ops:
  0.6 10.7 %copy-start.1 = (f32[1,1024]{1,0:T(1,128)S(1)}, f32[1,1024]{1,0:T(1,128)}, u32[]{:S(2)}) copy-start(f32[1,1024]{1,0:T(1,128)} %upwind.3) | copy-start | bytes 12292
  0.6 10.7 %copy-start = (bf16[1,12,25,1024]{3,2,1,0:T(8,128)(2,1)S(1)}, bf16[1,12,25,1024]{3,2,1,0:T(8,128)(2,1)}, u32[]{:S(2)}) copy-start(bf16[1,12,25,1024]{3,2,1,0:T(8,128)(2,1)} %jacobian.3) | copy-start | bytes 1843204
  13.8 11.2 %collective-permute-start = (f32[30,8,128]{2,1,0:T(8,128)S(1)}, f32[30,8,128]{2,1,0:T(8,128)S(1)}, u32[]{:S(2)}, u32[]{:S(2)}) collective-permute-start(f32[30,8,128]{2,1,0:T(8,128)S(1)} %get-tuple-element.17), channel_id=1, source_target_pairs={{0,2},{1,3},{2,0},{3,1},{4,6},{5,7},{6,4},{7,5},{8,10},{9,11},{10,... | collective-permute-start | bytes 368648 | tf_op jit(solution)/shard_map/ppermute | solution.py:44
  15.8 12.3 %collective-permute-start.1 = (f32[30,8,128]{2,1,0:T(8,128)S(1)}, f32[30,8,128]{2,1,0:T(8,128)S(1)}, u32[]{:S(2)}, u32[]{:S(2)}) collective-permute-start(f32[30,8,128]{2,1,0:T(8,128)S(1)} %get-tuple-element.18), channel_id=1, source_target_pairs={{0,510},{1,511},{2,4},{3,5},{4,2},{5,3},{6,8},{7,9},{8,6},{9,7},{1... | collective-permute-start | bytes 368648 | tf_op jit(solution)/shard_map/ppermute | solution.py:44
